TPU v7x, 128 devices: a whole 4x4x4 slice. The times are simulated.
128 devices in a mesh: sym: 8 (over y, x_lo), row: 16 (over x_hi, z, core).
Axes of the slice: x: 4 (x_hi: 2, x_lo: 2; x = x_hi * 2 + x_lo), y: 4, z: 4, core: 2. Of those that a mesh axis runs over, the one named last changes fastest.
Arguments:
- inner_state: float32 [8, 6144, 128], P('sym', 'row'), may hold values from -6 to 6
- outer_state: float32 [8, 24, 128, 2048], P('sym', None, None, 'row'), may hold values from -6 to 6
- block_hamiltonian: bfloat16 [8, 6144, 6144], P('sym', 'row'), may hold values from -2 to 2, as said below
- dipole: bfloat16 [8, 6144, 6144], P('sym', 'row'), may hold values from -0.078125 to 0.078125
- field_strength: float32 [64], replicated, may hold values from -1.2 to 1.2
- dipole_links: int32 [7, 64], replicated, may hold values 0 or 1
- ghost_amplitude: float32 [8, 2, 6144], P('sym'), may hold values from -0.4 to 0.4
- surface_amplitude: float32 [8, 6144], P('sym'), may hold values from -3 to 3
- state_channel: int32 [8, 6144], P('sym'), may hold values from 0 to 23
- threshold: float32 [8, 24], P('sym'), may hold values from 0 to 1
Outputs:
- inner_next: float32 [8, 6144, 128], P('sym', 'row')
- outer_next: float32 [8, 24, 128, 2048], P('sym', None, None, 'row')
Inputs may be any that keep to these rules, and one draw needn't show every extreme that they name: `block_hamiltonian`: each block is a symmetric matrix.
All inputs are finite; a program needn't handle non-finite values.
Results may differ from a plain program's by a relative error of at most 0.0085.
Values may be sent and summed in bfloat16 or wider, within the bound.
A program may use at most 128 MiB of HBM per device.

v0:
```python
import jax
import jax.numpy as jnp
from jax import lax
from jax.sharding import PartitionSpec as P

TERMS = 4


time_step = 2.0
spacing = 1.5
radius_start = 20.0
charge = 1.0


def shifted(x, axis, by):
    length = lax.axis_size(axis)
    pairs = [(i, i + by) for i in range(length) if 0 <= i + by < length]
    return lax.ppermute(x, axis, pairs)


def padded_2(block, sides, width):
    for axis, dim in sides:
        count = lax.axis_size(axis)
        forward = [(i, i + 1) for i in range(count - 1)]
        backward = [(target, source) for source, target in forward]
        low = lax.ppermute(
            lax.slice_in_dim(block, block.shape[dim] - width, None, axis=dim), axis, forward
        )
        high = lax.ppermute(lax.slice_in_dim(block, 0, width, axis=dim), axis, backward)
        block = jnp.concatenate([low, block, high], axis=dim)
    return block


def from_root(x, axis, root):
    return lax.dynamic_index_in_dim(lax.all_gather(x, axis), root, 0, keepdims=False)


def rotate(values, factor, axis):
    real_part, imag_part = jnp.split(values, 2, axis=axis)
    return jnp.concatenate([factor * imag_part, -factor * real_part], axis=axis)


def per_device(
    inner_state,
    outer_state,
    block_hamiltonian,
    dipole,
    field_strength,
    dipole_links,
    ghost_amplitude,
    surface_amplitude,
    state_channel,
    threshold,
):
    hamiltonian_rows = block_hamiltonian[0]
    dipole_rows = dipole[0]
    rows_here, all_states = hamiltonian_rows.shape
    channel_count = threshold.shape[1]
    radial_here = outer_state.shape[3]
    block_index = lax.axis_index("sym")
    row_index = lax.axis_index("row")
    block_total = dipole_links.shape[0] + 1
    link_row = lax.dynamic_index_in_dim(
        dipole_links, jnp.minimum(block_index, block_total - 2), 0, keepdims=False
    ).astype(jnp.float32)
    link_row = jnp.where(block_index == block_total - 1, jnp.zeros_like(link_row), link_row)
    coupled = jnp.concatenate([link_row, link_row])
    column_field = jnp.concatenate([field_strength, field_strength])
    channel_hot = (
        state_channel[0][:, None] == jnp.arange(channel_count, dtype=jnp.int32)[None, :]
    ).astype(jnp.float32)
    own_hot = lax.dynamic_slice_in_dim(channel_hot, row_index * rows_here, rows_here, 0)
    own_surface = lax.dynamic_slice_in_dim(
        surface_amplitude[0], row_index * rows_here, rows_here, 0
    )
    ghost_rows = ghost_amplitude[0]
    radius = radius_start + spacing * (
        row_index * radial_here + jnp.arange(radial_here, dtype=jnp.int32)
    ).astype(jnp.float32)
    potential = threshold[0][:, None] - charge / radius[None, :]
    first_slab = row_index == 0
    dipole_cols = None
    dipole_cols = lax.all_to_all(dipole_rows, "row", split_axis=1, concat_axis=0, tiled=True)
    inner_vec = inner_state[0]
    outer_vec = outer_state[0]
    inner_total = inner_vec
    outer_total = outer_vec
    for order in range(1, TERMS + 1):
        rounded = inner_vec.astype(jnp.bfloat16)
        from_above = shifted(rounded, "sym", -1)
        own_piece = lax.all_gather(rounded, "row", axis=0, tiled=True)
        upper_piece = lax.all_gather(from_above, "row", axis=0, tiled=True)
        hamiltonian_part = jnp.dot(hamiltonian_rows, own_piece, preferred_element_type=jnp.float32)
        upper_part = jnp.dot(dipole_rows, upper_piece, preferred_element_type=jnp.float32)
        weighted = channel_hot[None, :, :] * ghost_rows[:, :, None]
        ghost = jnp.einsum(
            "jpc,pq->jcq", weighted, own_piece.astype(jnp.float32), precision=lax.Precision.HIGHEST
        )
        lifted = lax.dot_general(
            dipole_cols, own_piece, (((0,), (0,)), ((), ())), preferred_element_type=jnp.float32
        )
        hamiltonian_part, upper_part, ghost, lifted = (hamiltonian_part, upper_part, ghost, lifted)
        lifted = lifted * coupled[None, :]
        lower_part = shifted(lifted.astype(jnp.bfloat16), "sym", 1).astype(lifted.dtype)
        padded = padded_2(outer_vec.astype(jnp.bfloat16), (("row", 2),), 2).astype(outer_vec.dtype)
        ghost_cols = jnp.stack([ghost[1], ghost[0]], axis=-1)
        lower_cols = jnp.where(first_slab, ghost_cols, padded[..., :2])
        padded = jnp.concatenate([lower_cols, padded[..., 2:]], axis=-1)
        laplace = (
            -padded[..., :-4]
            + 16.0 * padded[..., 1:-3]
            - 30.0 * padded[..., 2:-2]
            + 16.0 * padded[..., 3:-1]
            - padded[..., 4:]
        ) / (12.0 * spacing * spacing)
        outer_image = -0.5 * laplace + potential[:, None, :] * outer_vec
        slope = (outer_vec[..., 1] - ghost[0]) / (2.0 * spacing)
        slope = from_root(slope, "row", 0)
        source = jnp.dot(own_hot, slope, precision=lax.Precision.HIGHEST)
        inner_image = (
            hamiltonian_part
            + column_field[None, :] * (coupled[None, :] * upper_part + lower_part)
            + 0.5 * own_surface[:, None] * source
        )
        factor = time_step / order
        inner_vec = rotate(inner_image, factor, 1)
        outer_vec = rotate(outer_image, factor, 1)
        inner_total = inner_total + inner_vec
        outer_total = outer_total + outer_vec
    return (inner_total[None], outer_total[None])


def solution(mesh):
    return jax.shard_map(
        per_device,
        mesh=mesh,
        in_specs=(
            P("sym", "row", None),
            P("sym", None, None, "row"),
            P("sym", "row", None),
            P("sym", "row", None),
            P(),
            P(),
            P("sym", None, None),
            P("sym", None),
            P("sym", None),
            P("sym", None),
        ),
        out_specs=(P("sym", "row", None), P("sym", None, None, "row")),
        check_vma=False,
    )
```

profile of v0, /device:TPU:1, one launch (start us, length us, event | category | flops | bytes accessed | tf_op | source)
XLA Modules:
  0.0 454.4 jit_solution(4584209563427411953)
XLA Ops:
  8.8 6.6 %copy.41 = bf16[1,384,6144]{1,2,0:T(8,128)(2,1)} copy(bf16[1,384,6144]{2,1,0:T(8,128)(2,1)} %param.13) | data formatting | bytes 9437184 | tf_op args[3]
  15.5 9.4 %all-to-all-start = ((bf16[384,16,384]{0,2,1:T(8,128)(2,1)}), bf16[384,16,384]{0,2,1:T(8,128)(2,1)}, u32[]{:S(2)}, u32[]{:S(2)}) async-start(bf16[384,16,384]{0,2,1:T(8,128)(2,1)} %bitcast.245), calls=%async_computation | async-start | bytes 9437184 | tf_op jit(solution)/shard_map/all_to_all | solution.py:83
  29.0 62.2 %collective-permute-done = bf16[384,128]{1,0:T(8,128)(2,1)} collective-permute-done((bf16[384,128]{1,0:T(8,128)(2,1)}, bf16[384,128]{1,0:T(8,128)(2,1)}, u32[]{:S(2)}, u32[]{:S(2)}) %collective-permute-start) | collective-permute-done | bytes 98336 | tf_op jit(solution)/shard_map/ppermute | solution.py:18
  92.1 8.6 %all-gather.24.cloned.1.call-done = bf16[1,6144,128]{2,1,0:T(8,128)(2,1)} async-done(((bf16[1,384,128]{2,1,0:T(8,128)(2,1)}), bf16[1,6144,128]{2,1,0:T(8,128)(2,1)}) %all-gather.24.cloned.1.call-update) | async-done | bytes 1572880 | tf_op jit(solution)/shard_map/all_gather | solution.py:91
  103.0 27.1 %all_gather.42 = f32[16,24,128]{2,1,0:T(8,128)} all-gather(f32[1,24,128]{2,1,0:T(8,128)S(1)} %get-tuple-element.56), channel_id=1, replica_groups=mesh['sym'=8,'row'=16] {'row'}, dimensions={0}, use_global_device_ids=true | all-gather | bytes 208896 | tf_op jit(solution)/shard_map/all_gather | solution.py:35
  130.2 4.5 fusion.14
  134.7 6.8 %copy.42 = bf16[16,384,384]{2,1,0:T(8,128)(2,1)} copy(bf16[16,384,384]{1,2,0:T(8,128)(2,1)} %bitcast.6) | data formatting | bytes 9437184 | tf_op jit(solution)/shard_map/all_to_all | solution.py:83
  141.4 4.0 fusion.156
  145.5 3.6 collective-permute-start.1
  150.1 4.3 all-gather.10.cloned.1.call-done
  154.3 4.3 fusion.123
  162.1 3.0 collective-permute-start.4
  174.5 29.3 %all-gather.12.cloned.1.call-done = bf16[6144,128]{0,1:T(8,128)(2,1)} async-done(((bf16[384,128]{0,1:T(8,128)(2,1)}), bf16[6144,128]{0,1:T(8,128)(2,1)}) %all-gather.12.cloned.1.call-update) | async-done | bytes 1572880 | tf_op jit(solution)/shard_map/all_gather | solution.py:91
  203.8 3.9 fusion.161
  212.5 23.1 %all_gather.45 = f32[16,24,128]{2,1,0:T(8,128)S(1)} all-gather(f32[1,24,128]{2,1,0:T(8,128)S(1)} %get-tuple-element.53), channel_id=1, replica_groups=mesh['sym'=8,'row'=16] {'row'}, dimensions={0}, use_global_device_ids=true | all-gather | bytes 208896 | tf_op jit(solution)/shard_map/all_gather | solution.py:35
  235.7 4.5 fusion.75
  241.9 8.1 %all-gather.14.cloned.1.call-done = bf16[6144,128]{0,1:T(8,128)(2,1)} async-done(((bf16[384,128]{0,1:T(8,128)(2,1)}), bf16[6144,128]{0,1:T(8,128)(2,1)}) %all-gather.14.cloned.1.call-update) | async-done | bytes 1572880 | tf_op jit(solution)/shard_map/all_gather | solution.py:92
  250.0 4.4 fusion.132
  257.2 5.1 %collective-permute-done.6 = bf16[384,128]{0,1:T(8,128)(2,1)} collective-permute-done((bf16[384,128]{0,1:T(8,128)(2,1)}, bf16[384,128]{0,1:T(8,128)(2,1)}, u32[]{:S(2)}, u32[]{:S(2)}) %collective-permute-start.6) | collective-permute-done | bytes 98336 | tf_op jit(solution)/shard_map/ppermute | solution.py:18
  268.9 3.1 collective-permute-done.9
  277.6 22.3 %all-gather.16.cloned.1.call-done = bf16[6144,128]{0,1:T(8,128)(2,1)} async-done(((bf16[384,128]{0,1:T(8,128)(2,1)}), bf16[6144,128]{0,1:T(8,128)(2,1)}) %all-gather.16.cloned.1.call-update) | async-done | bytes 1572880 | tf_op jit(solution)/shard_map/all_gather | solution.py:91
  299.9 4.6 %fusion.160 = bf16[384,128]{0,1:T(8,128)(2,1)} fusion(bf16[6144,128]{0,1:T(8,128)(2,1)} %all-gather.16.cloned.1.call-done, bf16[6144,384]{1,0:T(8,128)(2,1)} %bitcast.242, f32[128]{0:T(128)S(1)} %pad_maximum_fusion.11), kind=kOutput, calls=%fused_computation.148 | convolution fusion | flops 604078080 | bytes 6390272 | tf_op jit(solution)/shard_map/dot_general | solution.py:99
  309.2 22.9 %all_gather.48 = f32[16,24,128]{2,1,0:T(8,128)S(1)} all-gather(f32[1,24,128]{2,1,0:T(8,128)S(1)} %get-tuple-element.50), channel_id=1, replica_groups=mesh['sym'=8,'row'=16] {'row'}, dimensions={0}, use_global_device_ids=true | all-gather | bytes 208896 | tf_op jit(solution)/shard_map/all_gather | solution.py:35
  332.2 4.5 fusion.78
  338.4 7.8 %all-gather.18.cloned.1.call-done = bf16[6144,128]{0,1:T(8,128)(2,1)} async-done(((bf16[384,128]{0,1:T(8,128)(2,1)}), bf16[6144,128]{0,1:T(8,128)(2,1)}) %all-gather.18.cloned.1.call-update) | async-done | bytes 1572880 | tf_op jit(solution)/shard_map/all_gather | solution.py:92
  346.1 4.4 fusion.141
  378.2 17.8 %all-gather.20.cloned.1.call-done = bf16[6144,128]{0,1:T(8,128)(2,1)} async-done(((bf16[384,128]{0,1:T(8,128)(2,1)}), bf16[6144,128]{0,1:T(8,128)(2,1)}) %all-gather.20.cloned.1.call-update) | async-done | bytes 1572880 | tf_op jit(solution)/shard_map/all_gather | solution.py:91
  396.0 4.6 %fusion.159 = bf16[384,128]{0,1:T(8,128)(2,1)} fusion(bf16[6144,128]{0,1:T(8,128)(2,1)} %all-gather.20.cloned.1.call-done, bf16[6144,384]{1,0:T(8,128)(2,1)} %bitcast.243, f32[128]{0:T(128)S(1)} %pad_maximum_fusion.11), kind=kOutput, calls=%fused_computation.147 | convolution fusion | flops 604078080 | bytes 6390272 | tf_op jit(solution)/shard_map/dot_general | solution.py:99
  400.6 3.0 collective-permute-start.11
  405.4 23.1 %all_gather.51 = f32[16,24,128]{2,1,0:T(8,128)S(1)} all-gather(f32[1,24,128]{2,1,0:T(8,128)S(1)} %get-tuple-element.47), channel_id=1, replica_groups=mesh['sym'=8,'row'=16] {'row'}, dimensions={0}, use_global_device_ids=true | all-gather | bytes 208896 | tf_op jit(solution)/shard_map/all_gather | solution.py:35
  438.4 3.9 all-gather.22.cloned.1.call-done
  442.2 4.3 fusion.150
  (201 shorter events, 90.4 us)
Async XLA Ops:
  7.2 93.5 %all-gather.24.cloned.1.call-start = ((), (), s32[]{:S(2)}) async-start(), calls=%async_computation.8 | async-start | bytes 1671168 | tf_op jit(solution)/shard_map/all_gather | solution.py:91
  15.5 119.2 %all-to-all-start = ((bf16[384,16,384]{0,2,1:T(8,128)(2,1)}), bf16[384,16,384]{0,2,1:T(8,128)(2,1)}, u32[]{:S(2)}, u32[]{:S(2)}) async-start(bf16[384,16,384]{0,2,1:T(8,128)(2,1)} %bitcast.245), calls=%async_computation | async-start | bytes 9437184 | tf_op jit(solution)/shard_map/all_to_all | solution.py:83
  24.9 129.4 %all-gather.10.cloned.1.call-start = ((), (), s32[]{:S(2)}) async-start(), calls=%async_computation.1 | async-start | bytes 1671168 | tf_op jit(solution)/shard_map/all_gather | solution.py:92
  25.6 65.6 %collective-permute-start = (bf16[384,128]{1,0:T(8,128)(2,1)}, bf16[384,128]{1,0:T(8,128)(2,1)}, u32[]{:S(2)}, u32[]{:S(2)}) collective-permute-start(bf16[384,128]{1,0:T(8,128)(2,1)} %convert_bitcast_fusion), channel_id=1, source_target_pairs={{16,0},{32,16},{48,32},{64,48},{80,64},{96,80},{112,96},{17,1},{33... | collective-permute-start | bytes 294920 | tf_op jit(solution)/shard_map/ppermute | solution.py:18
  26.9 64.4 %copy-start.41 = (s32[1,6144]{1,0:T(1,128)S(1)}, s32[1,6144]{1,0:T(1,128)}, u32[]{:S(2)}) copy-start(s32[1,6144]{1,0:T(1,128)} %param.18) | copy-start | bytes 73732
  26.9 73.7 %copy-start.30 = (f32[1,2,6144]{2,1,0:T(2,128)S(1)}, f32[1,2,6144]{2,1,0:T(2,128)}, u32[]{:S(2)}) copy-start(f32[1,2,6144]{2,1,0:T(2,128)} %param.16) | copy-start | bytes 147460
  91.2 112.6 %all-gather.12.cloned.1.call-start = ((), (), s32[]{:S(2)}) async-start(), calls=%async_computation.2 | async-start | bytes 1671168 | tf_op jit(solution)/shard_map/all_gather | solution.py:91
  92.1 42.6 %copy-start.10 = (f32[6144,24]{0,1:T(8,128)}, f32[6144,24]{0,1:T(8,128)S(1)}, u32[]{:S(2)}) copy-start(f32[6144,24]{0,1:T(8,128)S(1)} %get-tuple-element.58) | copy-start | bytes 1769476
  100.7 29.5 %copy-start.19 = (bf16[1,6144,128]{2,1,0:T(8,128)(2,1)S(1)}, bf16[1,6144,128]{2,1,0:T(8,128)(2,1)}, u32[]{:S(2)}) copy-start(bf16[1,6144,128]{2,1,0:T(8,128)(2,1)} %all-gather.24.cloned.1.call-done) | copy-start | bytes 4718596
  145.5 8.9 %collective-permute-start.1 = (bf16[384,128]{0,1:T(8,128)(2,1)}, bf16[384,128]{0,1:T(8,128)(2,1)S(1)}, u32[]{:S(2)}, u32[]{:S(2)}) collective-permute-start(bf16[384,128]{0,1:T(8,128)(2,1)} %fusion.156), channel_id=1, source_target_pairs={{0,16},{16,32},{32,48},{48,64},{64,80},{80,96},{96,112},{1,17},{17... | collective-permute-start | bytes 294920 | tf_op jit(solution)/shard_map/ppermute | solution.py:18
  160.0 90.0 %all-gather.14.cloned.1.call-start = ((), (), s32[]{:S(2)}) async-start(), calls=%async_computation.3 | async-start | bytes 1671168 | tf_op jit(solution)/shard_map/all_gather | solution.py:92
  160.8 6.3 %collective-permute-start.2 = (bf16[384,128]{0,1:T(8,128)(2,1)S(1)}, bf16[384,128]{0,1:T(8,128)(2,1)S(1)}, u32[]{:S(2)}, u32[]{:S(2)}) collective-permute-start(bf16[384,128]{0,1:T(8,128)(2,1)S(1)} %copy-done.34), channel_id=1, source_target_pairs={{16,0},{32,16},{48,32},{64,48},{80,64},{96,80},{112,96},{17,1},{33... | collective-permute-start | bytes 294920 | tf_op jit(solution)/shard_map/ppermute | solution.py:18
  162.1 5.8 %collective-permute-start.4 = (bf16[24,128,2]{1,0,2:T(8,128)(2,1)S(1)}, bf16[24,128,2]{1,0,2:T(8,128)(2,1)S(1)}, u32[]{:S(2)}, u32[]{:S(2)}) collective-permute-start(bf16[24,128,2]{1,0,2:T(8,128)(2,1)S(1)} %get-tuple-element.30), channel_id=1, source_target_pairs={{0,1},{1,2},{2,3},{3,4},{4,5},{5,6},{6,7},{7,8},{8,9},{9,10},{10,1... | collective-permute-start | bytes 36872 | tf_op jit(solution)/shard_map/ppermute | solution.py:26
  165.2 5.0 %collective-permute-start.5 = (bf16[24,128,2]{1,0,2:T(8,128)(2,1)S(1)}, bf16[24,128,2]{1,0,2:T(8,128)(2,1)S(1)}, u32[]{:S(2)}, u32[]{:S(2)}) collective-permute-start(bf16[24,128,2]{1,0,2:T(8,128)(2,1)S(1)} %get-tuple-element.31), channel_id=1, source_target_pairs={{1,0},{2,1},{3,2},{4,3},{5,4},{6,5},{7,6},{8,7},{9,8},{10,9},{11,1... | collective-permute-start | bytes 36872 | tf_op jit(solution)/shard_map/ppermute | solution.py:29
  167.8 132.1 %all-gather.16.cloned.1.call-start = ((), (), s32[]{:S(2)}) async-start(), calls=%async_computation.4 | async-start | bytes 1671168 | tf_op jit(solution)/shard_map/all_gather | solution.py:91
  207.8 34.1 %collective-permute-start.3 = (bf16[384,128]{0,1:T(8,128)(2,1)S(1)}, bf16[384,128]{0,1:T(8,128)(2,1)}, u32[]{:S(2)}, u32[]{:S(2)}) collective-permute-start(bf16[384,128]{0,1:T(8,128)(2,1)S(1)} %fusion.161), channel_id=1, source_target_pairs={{0,16},{16,32},{32,48},{48,64},{64,80},{80,96},{96,112},{1,17},{17... | collective-permute-start | bytes 294920 | tf_op jit(solution)/shard_map/ppermute | solution.py:18
  255.8 90.3 %all-gather.18.cloned.1.call-start = ((), (), s32[]{:S(2)}) async-start(), calls=%async_computation.5 | async-start | bytes 1671168 | tf_op jit(solution)/shard_map/all_gather | solution.py:92
  255.9 6.4 %collective-permute-start.6 = (bf16[384,128]{0,1:T(8,128)(2,1)}, bf16[384,128]{0,1:T(8,128)(2,1)}, u32[]{:S(2)}, u32[]{:S(2)}) collective-permute-start(bf16[384,128]{0,1:T(8,128)(2,1)} %pad_maximum_fusion.8), channel_id=1, source_target_pairs={{16,0},{32,16},{48,32},{64,48},{80,64},{96,80},{112,96},{17,1},{33... | collective-permute-start | bytes 294920 | tf_op jit(solution)/shard_map/ppermute | solution.py:18
  262.3 133.7 %all-gather.20.cloned.1.call-start = ((), (), s32[]{:S(2)}) async-start(), calls=%async_computation.6 | async-start | bytes 1671168 | tf_op jit(solution)/shard_map/all_gather | solution.py:91
  264.1 4.8 %collective-permute-start.8 = (bf16[24,128,2]{1,0,2:T(8,128)(2,1)S(1)}, bf16[24,128,2]{1,0,2:T(8,128)(2,1)S(1)}, u32[]{:S(2)}, u32[]{:S(2)}) collective-permute-start(bf16[24,128,2]{1,0,2:T(8,128)(2,1)S(1)} %get-tuple-element.28), channel_id=1, source_target_pairs={{0,1},{1,2},{2,3},{3,4},{4,5},{5,6},{6,7},{7,8},{8,9},{9,10},{10,1... | collective-permute-start | bytes 36872 | tf_op jit(solution)/shard_map/ppermute | solution.py:26
  266.9 5.0 %collective-permute-start.9 = (bf16[24,128,2]{1,0,2:T(8,128)(2,1)S(1)}, bf16[24,128,2]{1,0,2:T(8,128)(2,1)S(1)}, u32[]{:S(2)}, u32[]{:S(2)}) collective-permute-start(bf16[24,128,2]{1,0,2:T(8,128)(2,1)S(1)} %get-tuple-element.29), channel_id=1, source_target_pairs={{1,0},{2,1},{3,2},{4,3},{5,4},{6,5},{7,6},{8,7},{9,8},{10,9},{11,1... | collective-permute-start | bytes 36872 | tf_op jit(solution)/shard_map/ppermute | solution.py:29
  304.5 41.6 %collective-permute-start.7 = (bf16[384,128]{0,1:T(8,128)(2,1)}, bf16[384,128]{0,1:T(8,128)(2,1)}, u32[]{:S(2)}, u32[]{:S(2)}) collective-permute-start(bf16[384,128]{0,1:T(8,128)(2,1)} %fusion.160), channel_id=1, source_target_pairs={{0,16},{16,32},{32,48},{48,64},{64,80},{80,96},{96,112},{1,17},{17... | collective-permute-start | bytes 294920 | tf_op jit(solution)/shard_map/ppermute | solution.py:18
  351.9 90.3 %all-gather.22.cloned.1.call-start = ((), (), s32[]{:S(2)}) async-start(), calls=%async_computation.7 | async-start | bytes 1671168 | tf_op jit(solution)/shard_map/all_gather | solution.py:92
  353.8 4.3 collective-permute-start.12
  355.7 5.0 %collective-permute-start.13 = (bf16[24,128,2]{1,0,2:T(8,128)(2,1)S(1)}, bf16[24,128,2]{1,0,2:T(8,128)(2,1)S(1)}, u32[]{:S(2)}, u32[]{:S(2)}) collective-permute-start(bf16[24,128,2]{1,0,2:T(8,128)(2,1)S(1)} %get-tuple-element.27), channel_id=1, source_target_pairs={{1,0},{2,1},{3,2},{4,3},{5,4},{6,5},{7,6},{8,7},{9,8},{10,9},{11,1... | collective-permute-start | bytes 36872 | tf_op jit(solution)/shard_map/ppermute | solution.py:29
  367.5 6.5 %collective-permute-start.10 = (bf16[384,128]{0,1:T(8,128)(2,1)S(1)}, bf16[384,128]{0,1:T(8,128)(2,1)S(1)}, u32[]{:S(2)}, u32[]{:S(2)}) collective-permute-start(bf16[384,128]{0,1:T(8,128)(2,1)S(1)} %copy-done.33), channel_id=1, source_target_pairs={{16,0},{32,16},{48,32},{64,48},{80,64},{96,80},{112,96},{17,1},{33... | collective-permute-start | bytes 294920 | tf_op jit(solution)/shard_map/ppermute | solution.py:18
  368.8 5.8 %collective-permute-start.14 = (bf16[24,128,2]{1,0,2:T(8,128)(2,1)S(1)}, bf16[24,128,2]{1,0,2:T(8,128)(2,1)S(1)}, u32[]{:S(2)}, u32[]{:S(2)}) collective-permute-start(bf16[24,128,2]{1,0,2:T(8,128)(2,1)S(1)} %get-tuple-element.24), channel_id=1, source_target_pairs={{0,1},{1,2},{2,3},{3,4},{4,5},{5,6},{6,7},{7,8},{8,9},{9,10},{10,1... | collective-permute-start | bytes 36872 | tf_op jit(solution)/shard_map/ppermute | solution.py:26
  370.8 5.0 %collective-permute-start.15 = (bf16[24,128,2]{1,0,2:T(8,128)(2,1)S(1)}, bf16[24,128,2]{1,0,2:T(8,128)(2,1)S(1)}, u32[]{:S(2)}, u32[]{:S(2)}) collective-permute-start(bf16[24,128,2]{1,0,2:T(8,128)(2,1)S(1)} %get-tuple-element.25), channel_id=1, source_target_pairs={{1,0},{2,1},{3,2},{4,3},{5,4},{6,5},{7,6},{8,7},{9,8},{10,9},{11,1... | collective-permute-start | bytes 36872 | tf_op jit(solution)/shard_map/ppermute | solution.py:29
  400.6 37.8 %collective-permute-start.11 = (bf16[384,128]{0,1:T(8,128)(2,1)}, bf16[384,128]{0,1:T(8,128)(2,1)}, u32[]{:S(2)}, u32[]{:S(2)}) collective-permute-start(bf16[384,128]{0,1:T(8,128)(2,1)} %fusion.159), channel_id=1, source_target_pairs={{0,16},{16,32},{32,48},{48,64},{64,80},{80,96},{96,112},{1,17},{17... | collective-permute-start | bytes 294920 | tf_op jit(solution)/shard_map/ppermute | solution.py:18
  403.6 24.9 %copy-start.18 = (bf16[24,128,128]{1,0,2:T(8,128)(2,1)S(1)}, bf16[24,128,128]{1,0,2:T(8,128)(2,1)}, u32[]{:S(2)}) copy-start(bf16[24,128,128]{1,0,2:T(8,128)(2,1)} %copy-done.17) | copy-start | bytes 2359300
  405.3 23.2 %copy-start.1 = (f32[24,128,132]{1,0,2:T(8,128)S(1)}, f32[24,128,132]{1,0,2:T(8,128)}, u32[]{:S(2)}) copy-start(f32[24,128,132]{1,0,2:T(8,128)} %copy-done) | copy-start | bytes 4866052
  405.3 23.2 %slice-start.2 = ((f32[24,128,132]{1,0,2:T(8,128)}), f32[24,128,130]{1,0,2:T(8,128)S(1)}, s32[]{:S(2)}) async-start(f32[24,128,132]{1,0,2:T(8,128)} %copy-done), calls=%async_computation.11 | async-start | bytes 3194880 | tf_op jit(solution)/shard_map/slice | solution.py:108
  (40 other events, 197.3 us)
Sparse Core Ops, SparseCore 0:
  11.1 89.5 all-gather.23
  103.1 51.1 all-gather.9
  160.1 43.6 all-gather.11
  206.0 43.9 all-gather.13
  256.0 43.9 all-gather.15
  302.0 44.0 all-gather.17
  352.1 43.9 all-gather.19
  398.3 43.9 all-gather.21
where the time goes:
time: 456 us; the launch traced here: 454 us
  waiting for transfers between devices  178 us (39%)
  blocking collectives  96.3 us (21%)
  matrix products  62.3 us (14%)
  starting transfers between devices  45.7 us (10%)
  other arithmetic  29.9 us (7%)
  local copies, waits for them, and re-layouts  26.8 us (6%)
  between operations  15 us (3%)
    all_gather x4, blocking collectives, from_root(): lax.all_gather(x, axis)  96.3 us
    all_gather x4, waiting for transfers between devices, per_device(): own_piece = lax.all_gather(rounded, 'row', axis=0, tiled=True)  78 us
    ppermute x8, waiting for transfers between devices, shifted(): return lax.ppermute(x, axis, pairs)  67.2 us
    all_gather x4, waiting for transfers between devices, per_device(): upper_piece = lax.all_gather(from_above, 'row', axis=0, tiled=True)  24 us
    unnamed x97, local copies, waits for them, and re-layouts  19.7 us
    ppermute x8, starting transfers between devices, shifted(): return lax.ppermute(x, axis, pairs)  17.6 us
    dot_general x4, matrix products, per_device(): jnp.dot(dipole_rows, upper_piece, preferred_element_type=jnp.float32)  17.4 us
    dot_general x4, matrix products, per_device(): lax.dot_general(dipole_cols, own_piece, (((0,), (0,)), ((), ())), preferr...  17.2 us
  transfers between devices with their start and end apart: 25, of which 14 were waited for; matrix products, arithmetic and copies ran while one was open for 19% of the time, Pallas kernels for 0%

commit v1 on v0

v1 whole, which is shorter than its diff:
```python
import jax
import jax.numpy as jnp
from jax import lax
from jax.experimental import pallas as pl
from jax.experimental.pallas import tpu as pltpu
from jax.sharding import PartitionSpec as P

TERMS = 4
time_step = 2.0
spacing = 1.5
radius_start = 20.0
charge = 1.0

MESH = pl.DeviceIdType.MESH
BF = jnp.bfloat16
F32 = jnp.float32

ROWS = 384
HALF = 192
STATES = 6144
KHALF = 3072
CH = 24
Q = 128
SLAB = 128
S0 = 15.0 / (12.0 * spacing * spacing)
S1 = -8.0 / (12.0 * spacing * spacing)
S2 = 0.5 / (12.0 * spacing * spacing)


def kernel(
    inner_hbm, outer_hbm, ham_hbm, dip_hbm, par_ref, ghost_ref, surf_ref, chan_ref, edge_ref,
    total_ref, outer_ref,
    uf, uo, uu, ut, pt, rl, hp, hr, up, ur, hg, dc, sh, slp,
    tl, tr, dl, dr, cs, ct, ab, invr, ghs,
    ss, rs, es_s, es_r, as_s, as_r, ms_s, ms_r, ls,
):
    s = lax.axis_index("sym")
    r = lax.axis_index("row")
    xh = r // 8
    z = (r // 2) % 4
    c = r % 2
    me = xh * 4 + z
    deltas = (1, 3, 2)

    def zz(d, sign=1):
        return (z + sign * deltas[d] + 4) % 4

    def dev(b, x, zc):
        return (b, x * 8 + zc * 2 + c)

    below = (s + 7) % 8
    above = (s + 1) % 8
    partner = (s, xh * 8 + z * 2 + (1 - c))
    zdev = [dev(s, xh, zz(d)) for d in range(3)]
    xdev = dev(s, 1 - xh, z)

    cin = pltpu.make_async_copy(inner_hbm, uf, ls.at[0])
    cin.start()

    def own_cols(k, core):
        return pl.ds(pl.multiple_of((2 * k + core) * ROWS, ROWS), ROWS)

    crow = pl.ds(pl.multiple_of(c * ROWS, ROWS), ROWS)

    def local_mat(src, dst, k, sem):
        return pltpu.make_async_copy(
            src.at[:, own_cols(k, c)], dst.at[crow, pl.ds(k * ROWS, ROWS)], sem
        )

    def remote_mat(src, dst, k, i):
        return pltpu.make_async_remote_copy(
            src_ref=src.at[:, own_cols(k, 1 - c)], dst_ref=dst.at[crow, pl.ds(k * ROWS, ROWS)],
            send_sem=ms_s.at[i, k], recv_sem=ms_r.at[i, k], device_id=partner, device_id_type=MESH,
        )

    for k in range(8):
        local_mat(dip_hbm, dc, k, ls.at[8 + k]).start()

    barrier = pltpu.get_barrier_semaphore()
    for j in range(1, 16):
        pl.semaphore_signal(barrier, inc=1, device_id=(s, (r + j) % 16), device_id_type=MESH)
    for t in range(8):
        pl.semaphore_signal(barrier, inc=1, device_id=dev(above, t // 4, t % 4), device_id_type=MESH)
        pl.semaphore_signal(barrier, inc=1, device_id=dev(below, t // 4, t % 4), device_id_type=MESH)
    pl.semaphore_wait(barrier, 31)

    for k in range(8):
        remote_mat(dip_hbm, dc, k, 0).start()

    def rc(o, src, dst, si, ri, device):
        return pltpu.make_async_remote_copy(
            src_ref=src, dst_ref=dst, send_sem=ss.at[o, si], recv_sem=rs.at[o, ri],
            device_id=device, device_id_type=MESH,
        )

    lo = pl.ds(0, HALF)
    hi = pl.ds(HALF, HALF)
    ccol = pl.ds(pl.multiple_of(c * ROWS, ROWS), ROWS)

    def m_core(o):
        return rc(o, ut.at[o, :, ccol], ut.at[o, :, ccol], 0, 0, partner)

    def m_own(o, d):
        ref = uo.at[o, xh, z]
        return rc(o, ref, ref, 1 + d, 1 + d, zdev[d] if d < 3 else xdev)

    def m_up(o, x):
        return rc(o, uo.at[o, xh, z], uu.at[o, xh, z], 5 + x, 5 + xh, dev(below, x, z))

    def m_f1(o, d):
        ref = uo.at[o, 1 - xh, z, lo]
        return rc(o, ref, ref, 7 + d, 7 + d, zdev[d])

    def m_f2(o, d):
        ref = uo.at[o, xh, zz(d, -1), hi]
        return rc(o, ref, ref, 10 + d, 10 + d, xdev)

    def m_f2u(o, d, x):
        return rc(o, uo.at[o, xh, zz(d, -1), hi], uu.at[o, xh, zz(d, -1), hi],
                  13 + x * 3 + d, 13 + xh * 3 + d, dev(below, x, z))

    def m_f3(o, d):
        ref = uu.at[o, :, z, lo]
        return rc(o, ref, ref, 19 + d, 19 + d, zdev[d])

    def m_low(o, t):
        return rc(o, pt.at[o, t], rl.at[o, me], 22 + t, 22 + me, dev(above, t // 4, t % 4))

    def m_hp(o):
        return rc(o, hp.at[o, 1 - c], hr.at[o], 30, 30, partner)

    def m_upp(o):
        return rc(o, up.at[o, 1 - c], ur.at[o], 31, 31, partner)

    def wr(o, dst, ri):
        rc(o, dst, dst, ri, ri, partner).wait_recv()

    def all_msgs(o):
        out = [m_core(o)]
        out += [m_own(o, d) for d in range(4)]
        out += [m_up(o, x) for x in range(2)]
        out += [m_f1(o, d) for d in range(3)] + [m_f2(o, d) for d in range(3)]
        out += [m_f2u(o, d, x) for x in range(2) for d in range(3)]
        out += [m_f3(o, d) for d in range(3)]
        out += [m_low(o, t) for t in range(8)]
        return out + [m_hp(o), m_upp(o)]

    right = (s, (r + 1) % 16)
    left = (s, (r + 15) % 16)

    def m_edge(i):
        src = edge_ref.at[pl.ds(8, 8)] if i == 0 else edge_ref.at[pl.ds(0, 8)]
        dst = tl.at[pl.ds(0, 8)] if i == 0 else tr.at[pl.ds(8, 8)]
        return pltpu.make_async_remote_copy(
            src_ref=src, dst_ref=dst, send_sem=es_s.at[i], recv_sem=es_r.at[i],
            device_id=right if i == 0 else left, device_id_type=MESH,
        )

    def m_first(j):
        return pltpu.make_async_remote_copy(
            src_ref=ab, dst_ref=ab, send_sem=as_s.at[j], recv_sem=as_r,
            device_id=(s, j), device_id_type=MESH,
        )

    lane = lax.broadcasted_iota(jnp.int32, (1, Q), 1)
    sign = jnp.where(lane < Q // 2, F32(1.0), F32(-1.0))

    def spin(x):
        return pltpu.roll(x, Q // 2, 1) * sign

    cin.wait()

    pos = lax.broadcasted_iota(jnp.int32, (32, Q), 0)
    pos = jnp.where(pos < 16, pos - 8, pos + 104) + r * SLAB
    invr[...] = charge / (radius_start + spacing * pos.astype(F32))
    thr = par_ref[0:CH, :]

    def image(two_low, low, mid, high, two_high, inv):
        return S2 * (two_low + two_high) + S1 * (low + high) + (S0 + thr - inv) * mid

    def inv_first(p):
        return charge / (radius_start + spacing * p)

    def factor_of(o):
        return jnp.where(o == 0, F32(2.0), jnp.where(o == 1, F32(1.0), jnp.where(o == 2, F32(2.0 / 3.0), F32(0.5))))

    total_ref[...] = uf[...]

    def send_first(o):
        u = uf[...]
        uo[o, xh, z] = u.astype(BF)
        for d in range(4):
            m_own(o, d).start()
        for x in range(2):
            m_up(o, x).start()
        ut[o, :, ccol] = jnp.transpose(u).astype(BF)
        m_core(o).start()

    send_first(0)
    m_edge(0).start()
    m_edge(1).start()

    @pl.when(r == 0)
    def _():
        zero = jnp.zeros((CH, Q), F32)
        strip = [edge_ref[p] for p in range(8)]
        ab[0] = strip[1]
        for k in range(1, TERMS):
            keep = 8 - 2 * k
            ext = [zero, zero] + strip
            strip = [
                (time_step / k) * spin(image(ext[p], ext[p + 1], ext[p + 2], ext[p + 3], ext[p + 4], inv_first(p)))
                for p in range(keep)
            ]
            ab[k] = strip[1]
        for j in range(1, 16):
            m_first(j).start()

    for k in range(8):
        local_mat(ham_hbm, hg, k, ls.at[16 + k]).start()
        remote_mat(ham_hbm, hg, k, 1).start()
    cout = pltpu.make_async_copy(outer_hbm, outer_ref, ls.at[1])
    cout.start()

    for k in range(8):
        cols = own_cols(k, c)
        hot = chan_ref[0:1, cols] == lax.broadcasted_iota(jnp.int32, (CH, ROWS), 0)
        for j in range(2):
            g = jnp.where(hot, ghost_ref[j:j + 1, cols], F32(0.0))
            top = g.astype(BF)
            hg[768 + j * CH:768 + (j + 1) * CH, k * ROWS:(k + 1) * ROWS] = top
            hg[816 + j * CH:816 + (j + 1) * CH, k * ROWS:(k + 1) * ROWS] = (g - top.astype(F32)).astype(BF)
    mine = pl.ds(pl.multiple_of(r * ROWS, ROWS), ROWS)
    hot = chan_ref[0:1, mine] == lax.broadcasted_iota(jnp.int32, (Q, ROWS), 0)
    sh[...] = jnp.transpose(jnp.where(hot, 0.5 * surf_ref[0:1, mine], F32(0.0)))
    slp[...] = jnp.zeros_like(slp)
    for ref in (dl, dr, cs, ct):
        ref[...] = jnp.zeros_like(ref)
    tl[8:16] = edge_ref[0:8]
    tr[0:8] = edge_ref[8:16]

    col_upper = par_ref[CH:CH + 1, :]
    col_lower = par_ref[CH + 1:CH + 2, :]
    pos_lane = (lax.broadcasted_iota(jnp.int32, (1, SLAB), 1) + r * SLAB).astype(F32)
    lane_inv = charge / (radius_start + spacing * pos_lane)

    def outer_channel(ch):
        w = outer_ref[ch]
        acc = w
        mid = (S0 + par_ref[pl.ds(ch, 1), :]) - lane_inv
        for k in range(1, TERMS + 1):
            p1 = jnp.where(lane >= 1, pltpu.roll(w, 1, 1), 0.0)
            p2 = jnp.where(lane >= 2, pltpu.roll(w, 2, 1), 0.0)
            n1 = jnp.where(lane < SLAB - 1, pltpu.roll(w, SLAB - 1, 1), 0.0)
            n2 = jnp.where(lane < SLAB - 2, pltpu.roll(w, SLAB - 2, 1), 0.0)
            img = S2 * (p2 + n2) + S1 * (p1 + n1) + mid * w
            f = time_step / k
            w = jnp.concatenate([f * img[Q // 2:], -f * img[:Q // 2]], axis=0)
            acc = acc + w
        outer_ref[ch] = acc

    def order(o, carry):
        factor = factor_of(o)

        @pl.when(o > 0)
        def _():
            send_first(o)

        @pl.when(o == 0)
        def _():
            for k in range(8):
                local_mat(dip_hbm, dc, k, ls.at[8 + k]).wait()
                remote_mat(dip_hbm, dc, k, 0).wait_recv()

        wr(o, ut.at[o, :, ccol], 0)
        both = ut[o]
        for pair in range(4):
            prod = jnp.dot(both, dc[:, pair * 768:(pair + 1) * 768], preferred_element_type=F32)
            for j in range(2):
                pt[o, pair * 2 + j] = prod[:, j * ROWS:(j + 1) * ROWS].astype(BF)
                m_low(o, pair * 2 + j).start()

        for d in range(2):
            wr(o, uo.at[o, xh, zz(d, -1)], 1 + d)
            m_f2(o, d).start()
            for x in range(2):
                m_f2u(o, d, x).start()
        wr(o, uo.at[o, 1 - xh, z], 4)
        for d in range(3):
            m_f1(o, d).start()
        for x in range(2):
            wr(o, uu.at[o, x, z], 5 + x)
        for d in range(3):
            m_f3(o, d).start()
        wr(o, uo.at[o, xh, zz(2, -1)], 3)
        m_f2(o, 2).start()
        for x in range(2):
            m_f2u(o, 2, x).start()

        @pl.when(o == 0)
        def _():
            for k in range(8):
                local_mat(ham_hbm, hg, k, ls.at[16 + k]).wait()
                remote_mat(ham_hbm, hg, k, 1).wait_recv()
            cout.wait()
            m_edge(0).wait_recv()
            m_edge(1).wait_recv()

        def chans(j, carry):
            outer_channel(o * 6 + j)
            return carry

        lax.fori_loop(0, 6, chans, 0)

        for d in range(3):
            wr(o, uo.at[o, 1 - xh, zz(d, -1), lo], 7 + d)
            wr(o, uo.at[o, 1 - xh, zz(d, -1), hi], 10 + d)
        prod = jnp.dot(hg[...], uo[o].reshape(KHALF, Q), preferred_element_type=F32)
        gpart = prod[768:816] + prod[816:864]
        for j in range(2):
            hp[o, j, 0:ROWS] = prod[j * ROWS:(j + 1) * ROWS]
            hp[o, j, ROWS:ROWS + 48] = gpart
        m_hp(o).start()

        for d in range(3):
            for x in range(2):
                wr(o, uu.at[o, x, zz(d, -1), hi], 13 + x * 3 + d)
            wr(o, uu.at[o, :, zz(d, -1), lo], 19 + d)
        prod = jnp.dot(dc[...], uu[o].reshape(KHALF, Q), preferred_element_type=F32)
        for j in range(2):
            up[o, j] = prod[j * ROWS:(j + 1) * ROWS]
        m_upp(o).start()

        wr(o, hr.at[o], 30)
        ghs[...] = hr[o, ROWS:ROWS + 48] + hp[o, c, ROWS:ROWS + 48]
        ghost0 = ghs[0:CH]
        ghost1 = ghs[CH:2 * CH]

        @pl.when((o == 0) & (r != 0))
        def _():
            m_first(1).wait_recv()

        slp[0:CH] = (ab[o] + cs[3] - ghost0) * (1.0 / (2.0 * spacing))
        source = jnp.dot(sh[...], slp[...], precision=lax.Precision.HIGHEST, preferred_element_type=F32)
        first = r == 0
        last = r == 15
        dl[0] = jnp.where(first, ghost1, tl[6])
        dl[1] = jnp.where(first, ghost0, tl[7])
        dr[10] = jnp.where(last, 0.0, tr[8])
        dr[11] = jnp.where(last, 0.0, tr[9])
        cs[0] = ghost1
        cs[1] = ghost0

        def advance(ref, first_index, count, inv):
            out = [
                factor * spin(image(ref[i - 2], ref[i - 1], ref[i], ref[i + 1], ref[i + 2], inv(i)))
                for i in range(first_index, first_index + count)
            ]
            for i in range(count):
                ref[first_index + i] = out[i]

        advance(tl, 2, 12, lambda i: invr[i:i + 1, :])
        advance(tr, 2, 12, lambda i: invr[16 + i:17 + i, :])
        advance(dl, 2, 8, lambda i: invr[6 + i:7 + i, :])
        advance(dr, 2, 8, lambda i: invr[14 + i:15 + i, :])
        advance(cs, 2, 8, lambda i: inv_first(i - 2))
        ct[0:8] = ct[0:8] + dl[2:10]
        ct[8:16] = ct[8:16] + dr[2:10]

        for k in range(8):
            wr(o, rl.at[o, k], 22 + k)
        low = rl[o, 0].astype(F32)
        for k in range(1, 8):
            low = low + rl[o, k].astype(F32)
        low = jnp.transpose(low)
        wr(o, ur.at[o], 31)
        img = (
            hp[o, c, 0:ROWS] + hr[o, 0:ROWS] + source
            + col_upper * (up[o, c] + ur[o])
            + jnp.where(s == 0, 0.0, col_lower * low)
        )
        new = factor * spin(img)
        uf[...] = new
        total_ref[...] = total_ref[...] + new
        return carry

    lax.fori_loop(0, TERMS, order, 0)

    def fix(ch, carry):
        rows = ct[:, pl.ds(ch, 1), :].reshape(16, Q)
        block = jnp.concatenate([rows[0:8], jnp.zeros((SLAB - 16, Q), F32), rows[8:16]], axis=0)
        outer_ref[ch] = outer_ref[ch] + jnp.transpose(block)
        return carry

    lax.fori_loop(0, CH, fix, 0)

    def drain(o, carry):
        for m in all_msgs(o):
            m.wait_send()
        return carry

    lax.fori_loop(0, TERMS, drain, 0)
    for k in range(8):
        remote_mat(dip_hbm, dc, k, 0).wait_send()
        remote_mat(ham_hbm, hg, k, 1).wait_send()
    m_edge(0).wait_send()
    m_edge(1).wait_send()

    @pl.when(r == 0)
    def _():
        for j in range(1, 16):
            m_first(j).wait_send()


def per_device(
    inner_state, outer_state, block_hamiltonian, dipole, field_strength, dipole_links,
    ghost_amplitude, surface_amplitude, state_channel, threshold,
):
    block_index = lax.axis_index("sym")
    links = jnp.pad(dipole_links.astype(F32), ((1, 1), (0, 0)))
    near = lax.dynamic_slice_in_dim(links, block_index, 2, 0)
    near = near[::-1] * field_strength[None, :]
    par = jnp.concatenate([
        jnp.broadcast_to(threshold[0][:, None], (CH, Q)),
        jnp.concatenate([near, near], axis=1),
        jnp.zeros((6, Q), F32),
    ], axis=0)
    outer = outer_state[0]
    edge = jnp.transpose(jnp.concatenate([outer[..., :8], outer[..., SLAB - 8:]], axis=-1), (2, 0, 1))
    any_ = pl.BlockSpec(memory_space=pl.ANY)
    vmem = pl.BlockSpec(memory_space=pltpu.VMEM)
    dma = pltpu.SemaphoreType.DMA
    inner_next, outer_next = pl.pallas_call(
        kernel,
        out_shape=(
            jax.ShapeDtypeStruct((ROWS, Q), F32),
            jax.ShapeDtypeStruct((CH, Q, SLAB), F32),
        ),
        in_specs=[any_] * 4 + [vmem] * 5,
        out_specs=(vmem, vmem),
        scratch_shapes=[
            pltpu.VMEM((ROWS, Q), F32),
            pltpu.VMEM((TERMS, 2, 4, ROWS, Q), BF),
            pltpu.VMEM((TERMS, 2, 4, ROWS, Q), BF),
            pltpu.VMEM((TERMS, Q, 2 * ROWS), BF),
            pltpu.VMEM((TERMS, 8, Q, ROWS), BF),
            pltpu.VMEM((TERMS, 8, Q, ROWS), BF),
            pltpu.VMEM((TERMS, 2, ROWS + 48, Q), F32),
            pltpu.VMEM((TERMS, ROWS + 48, Q), F32),
            pltpu.VMEM((TERMS, 2, ROWS, Q), F32),
            pltpu.VMEM((TERMS, ROWS, Q), F32),
            pltpu.VMEM((864, KHALF), BF),
            pltpu.VMEM((768, KHALF), BF),
            pltpu.VMEM((ROWS, Q), F32),
            pltpu.VMEM((Q, Q), F32),
            pltpu.VMEM((16, CH, Q), F32),
            pltpu.VMEM((16, CH, Q), F32),
            pltpu.VMEM((12, CH, Q), F32),
            pltpu.VMEM((12, CH, Q), F32),
            pltpu.VMEM((12, CH, Q), F32),
            pltpu.VMEM((16, CH, Q), F32),
            pltpu.VMEM((TERMS, CH, Q), F32),
            pltpu.VMEM((32, Q), F32),
            pltpu.VMEM((48, Q), F32),
            dma((TERMS, 32)), dma((TERMS, 32)),
            dma((2,)), dma((2,)),
            dma((16,)), dma,
            dma((2, 8)), dma((2, 8)),
            dma((24,)),
        ],
        compiler_params=pltpu.CompilerParams(
            collective_id=0, has_side_effects=True, vmem_limit_bytes=52 * 1024 * 1024
        ),
        name="propagate",
    )(
        inner_state[0], outer, block_hamiltonian[0], dipole[0], par,
        ghost_amplitude[0], surface_amplitude, state_channel, edge,
    )
    return inner_next[None], outer_next[None]


def solution(mesh):
    return jax.shard_map(
        per_device,
        mesh=mesh,
        in_specs=(
            P("sym", "row", None),
            P("sym", None, None, "row"),
            P("sym", "row", None),
            P("sym", "row", None),
            P(),
            P(),
            P("sym", None, None),
            P("sym", None),
            P("sym", None),
            P("sym", None),
        ),
        out_specs=(P("sym", "row", None), P("sym", None, None, "row")),
        check_vma=False,
    )
```

time: 456 us -> 168 us (0.37)
  waiting for transfers between devices: 178 us -> 0 us
  Pallas kernels: 0 us -> 157 us
  blocking collectives: 96.3 us -> 0 us
  matrix products: 62.3 us -> 0 us
  starting transfers between devices: 45.7 us -> 0 us
  other arithmetic: 29.9 us -> 1.43 us
  local copies, waits for them, and re-layouts: 26.8 us -> 6.2 us
  between operations: 15 us -> 0.73 us
    pallas_call x0 -> x1, Pallas kernels: none -> 157 us  [per_device(): pl.pallas_call(kernel, out_shape=(jax.ShapeDtypeStruct((ROWS, Q), F32), j...]
    all_gather x8 -> x0, waiting for transfers between devices: 102 us -> none  [the longest x4 78 us: per_device(): own_piece = lax.all_gather(rounded, 'row', axis=0, tiled=True)]
    all_gather x4 -> x0, blocking collectives: 96.3 us -> none  [from_root(): lax.all_gather(x, axis)]
    ppermute x16 -> x0, waiting for transfers between devices: 76.3 us -> none  [the longest x8 67.2 us: shifted(): return lax.ppermute(x, axis, pairs)]
    dot_general x20 -> x0, matrix products: 62.3 us -> none  [the longest x4 17.4 us: per_device(): jnp.dot(dipole_rows, upper_piece, preferred_element_type=jnp.float32)]
    ppermute x16 -> x0, starting transfers between devices: 35.9 us -> none  [the longest x8 17.6 us: shifted(): return lax.ppermute(x, axis, pairs)]
    unnamed x97 -> x11, local copies, waits for them, and re-layouts: 19.7 us -> 5.4 us
    concatenate x10 -> x1, other arithmetic: 10.6 us -> 0.07 us  [per_device(): jnp.concatenate([jnp.broadcast_to(threshold[0][:, None], (CH, Q)), jnp.co...]
  transfers between devices with their start and end apart: 25 -> 0, of which waited for: 14 -> 0; matrix products, arithmetic and copies ran while one was open for 19% -> 0% of each run, Pallas kernels for 0% -> 0%
where the time goes in v1:
time: 168 us; the launch traced here: 166 us
  Pallas kernels  157 us (93%)
  local copies, waits for them, and re-layouts  6.2 us (4%)
    pallas_call x1, Pallas kernels, per_device(): pl.pallas_call(kernel, out_shape=(jax.ShapeDtypeStruct((ROWS, Q), F32), j...  157 us
    unnamed x11, local copies, waits for them, and re-layouts  5.4 us

profile of v1, /device:TPU:1, one launch (start us, length us, event | category | flops | bytes accessed | tf_op | source)
XLA Modules:
  0.0 165.7 jit_solution(232776092298610289)
XLA Ops:
  0.6 0.7 pad.7.clone
  1.3 0.1 pad.10.clone
  1.4 0.7 convert_element_type.5
  2.1 0.7 broadcast_multiply_fusion
  2.8 0.1 maximum_maximum_fusion.par_ref
  2.8 0.0 copy-start
  2.8 0.0 copy-start.1
  2.8 0.0 copy-start.2
  2.9 0.0 copy-start.3
  2.9 2.0 %copy.12 = f32[1,24,128,128]{2,1,3,0:T(8,128)S(1)} copy(f32[1,24,128,128]{3,2,1,0:T(8,128)} %param.11) | data formatting | bytes 3145728 | tf_op args[1]
  4.9 0.0 copy-done
  4.9 0.0 copy-done.1
  4.9 0.0 copy-done.2
  5.0 0.0 copy-done.3
  5.0 157.3 %propagate.1 = (f32[384,128]{1,0:T(8,128)S(1)}, f32[24,128,128]{2,1,0:T(8,128)}) custom-call(f32[384,128]{1,0:T(8,128)S(1)} %bitcast.12, f32[24,128,128]{2,1,0:T(8,128)} %bitcast.14, bf16[384,6144]{1,0:T(8,128)(2,1)} %bitcast.15, bf16[384,6144]{1,0:T(8,128)(2,1)} %bitcast.16, f32[32,128]{1,0:T(8,128)S(1)} %maximum_maximum_fusion.par_ref, ...), custom_call_target="tpu_custom_call" | custom-call | tf_op jit(solution)/shard_map/propagate/pallas_call | solution.py:433
  162.3 0.7 copy.17
  163.0 2.7 %copy.18 = f32[1,24,128,128]{3,2,1,0:T(8,128)} copy(f32[1,24,128,128]{3,2,1,0:T(8,128)} %bitcast.18) | data formatting | bytes 3145728
  (5 shorter events, 0.1 us)
Async XLA Ops:
  2.8 2.1 %copy-start = (f32[1,384,128]{2,1,0:T(8,128)S(1)}, f32[1,384,128]{2,1,0:T(8,128)}, u32[]{:S(2)}) copy-start(f32[1,384,128]{2,1,0:T(8,128)} %param.10) | copy-start | bytes 589828
  2.8 2.1 %copy-start.1 = (f32[1,2,6144]{2,1,0:T(2,128)S(1)}, f32[1,2,6144]{2,1,0:T(2,128)}, u32[]{:S(2)}) copy-start(f32[1,2,6144]{2,1,0:T(2,128)} %param.16) | copy-start | bytes 147460
  2.8 2.1 %copy-start.2 = (f32[1,6144]{1,0:T(1,128)S(1)}, f32[1,6144]{1,0:T(1,128)}, u32[]{:S(2)}) copy-start(f32[1,6144]{1,0:T(1,128)} %surf_ref.1) | copy-start | bytes 73732
  2.9 2.1 %copy-start.3 = (s32[1,6144]{1,0:T(1,128)S(1)}, s32[1,6144]{1,0:T(1,128)}, u32[]{:S(2)}) copy-start(s32[1,6144]{1,0:T(1,128)} %chan_ref.1) | copy-start | bytes 73732

commit v2 on v1

--- a/solution.py
+++ b/solution.py
@@ -16,7 +16,7 @@
 F32 = jnp.float32
 
 ROWS = 384
-HALF = 192
+FIRST = 96
 STATES = 6144
 KHALF = 3072
 CH = 24
@@ -28,18 +28,22 @@
 
 
 def kernel(
-    inner_hbm, outer_hbm, ham_hbm, dip_hbm, par_ref, ghost_ref, surf_ref, chan_ref, edge_ref,
-    total_ref, outer_ref,
-    uf, uo, uu, ut, pt, rl, hp, hr, up, ur, hg, dc, sh, slp,
-    tl, tr, dl, dr, cs, ct, ab, invr, ghs,
-    ss, rs, es_s, es_r, as_s, as_r, ms_s, ms_r, ls,
+    inner_hbm, outer_hbm, ham_hbm, dip_hbm, *rest,
 ):
+    small_hbm, (total_hbm, outer_out, pack_hbm), scratch = rest[:6], rest[6:9], rest[9:]
+    small, scratch = scratch[:6], scratch[6:]
+    field_ref, link_ref, thr_ref, ghost_ref, surf_ref, chan_ref = small
+    (
+        total_ref, outer_ref, ct, pack,
+        uf, uo, uu, ut, pt, rfar, rz, rsum, rl, acc, hp, hr, up, ur, hg, dc, sh, slp,
+        edge_ref, thr_col, tl, tr, dl, dr, cs, ab, invr, ghs,
+        ss, rs, es_s, es_r, as_s, as_r, ms_s, ms_r, ls,
+    ) = scratch
     s = lax.axis_index("sym")
     r = lax.axis_index("row")
     xh = r // 8
     z = (r // 2) % 4
     c = r % 2
-    me = xh * 4 + z
     deltas = (1, 3, 2)
 
     def zz(d, sign=1):
@@ -56,6 +60,9 @@
 
     cin = pltpu.make_async_copy(inner_hbm, uf, ls.at[0])
     cin.start()
+    csmall = [pltpu.make_async_copy(small_hbm[i], small[i], ls.at[2 + i]) for i in range(6)]
+    for copy in csmall:
+        copy.start()
 
     def own_cols(k, core):
         return pl.ds(pl.multiple_of((2 * k + core) * ROWS, ROWS), ROWS)
@@ -75,14 +82,16 @@
 
     for k in range(8):
         local_mat(dip_hbm, dc, k, ls.at[8 + k]).start()
+    cout = pltpu.make_async_copy(outer_hbm, outer_ref, ls.at[1])
+    cout.start()
 
     barrier = pltpu.get_barrier_semaphore()
     for j in range(1, 16):
         pl.semaphore_signal(barrier, inc=1, device_id=(s, (r + j) % 16), device_id_type=MESH)
-    for t in range(8):
-        pl.semaphore_signal(barrier, inc=1, device_id=dev(above, t // 4, t % 4), device_id_type=MESH)
-        pl.semaphore_signal(barrier, inc=1, device_id=dev(below, t // 4, t % 4), device_id_type=MESH)
-    pl.semaphore_wait(barrier, 31)
+    for x in range(2):
+        pl.semaphore_signal(barrier, inc=1, device_id=dev(above, x, z), device_id_type=MESH)
+        pl.semaphore_signal(barrier, inc=1, device_id=dev(below, x, z), device_id_type=MESH)
+    pl.semaphore_wait(barrier, 19)
 
     for k in range(8):
         remote_mat(dip_hbm, dc, k, 0).start()
@@ -93,8 +102,8 @@
             device_id=device, device_id_type=MESH,
         )
 
-    lo = pl.ds(0, HALF)
-    hi = pl.ds(HALF, HALF)
+    lo = pl.ds(0, FIRST)
+    hi = pl.ds(FIRST, ROWS - FIRST)
     ccol = pl.ds(pl.multiple_of(c * ROWS, ROWS), ROWS)
 
     def m_core(o):
@@ -123,8 +132,20 @@
         ref = uu.at[o, :, z, lo]
         return rc(o, ref, ref, 19 + d, 19 + d, zdev[d])
 
-    def m_low(o, t):
-        return rc(o, pt.at[o, t], rl.at[o, me], 22 + t, 22 + me, dev(above, t // 4, t % 4))
+    half = Q // 2
+    part = (pl.ds(0, half), pl.ds(half, half))
+
+    def m_far(o, d):
+        return rc(o, pt.at[o, :, zz(2), part[d]], rfar.at[o, d], 22 + d, 22 + d, zdev[d])
+
+    def m_near(o, d):
+        return rc(o, pt.at[o, :, zz(d), part[1 - d]], rz.at[o, d, :, part[1 - d]], 27 + d, 27 + d, zdev[d])
+
+    def m_both(o, d):
+        return rc(o, pt.at[o, :, zz(d), part[d]], rz.at[o, d, :, part[d]], 32 + d, 32 + d, zdev[d])
+
+    def m_lowx(o, x):
+        return rc(o, rsum.at[o, x], rl.at[o, xh], 25 + x, 25 + xh, dev(above, x, z))
 
     def m_hp(o):
         return rc(o, hp.at[o, 1 - c], hr.at[o], 30, 30, partner)
@@ -142,7 +163,7 @@
         out += [m_f1(o, d) for d in range(3)] + [m_f2(o, d) for d in range(3)]
         out += [m_f2u(o, d, x) for x in range(2) for d in range(3)]
         out += [m_f3(o, d) for d in range(3)]
-        out += [m_low(o, t) for t in range(8)]
+        out += [m(o, d) for d in range(2) for m in (m_far, m_near, m_both, m_lowx)]
         return out + [m_hp(o), m_upp(o)]
 
     right = (s, (r + 1) % 16)
@@ -170,10 +191,16 @@
 
     cin.wait()
 
+    for copy in csmall:
+        copy.wait()
     pos = lax.broadcasted_iota(jnp.int32, (32, Q), 0)
     pos = jnp.where(pos < 16, pos - 8, pos + 104) + r * SLAB
     invr[...] = charge / (radius_start + spacing * pos.astype(F32))
-    thr = par_ref[0:CH, :]
+    square = (CH, CH)
+    eye = lax.broadcasted_iota(jnp.int32, square, 0) == lax.broadcasted_iota(jnp.int32, square, 1)
+    column = jnp.sum(jnp.where(eye, jnp.broadcast_to(thr_ref[0:1, :], square), 0.0), axis=1, keepdims=True)
+    thr_col[...] = jnp.broadcast_to(column, (CH, Q))
+    thr = thr_col[...]
 
     def image(two_low, low, mid, high, two_high, inv):
         return S2 * (two_low + two_high) + S1 * (low + high) + (S0 + thr - inv) * mid
@@ -197,6 +224,26 @@
         m_core(o).start()
 
     send_first(0)
+    for k in range(8):
+        local_mat(ham_hbm, hg, k, ls.at[16 + k]).start()
+        remote_mat(ham_hbm, hg, k, 1).start()
+    cout.wait()
+
+    def edges(g, carry):
+        block = jnp.zeros((Q, SLAB), F32)
+        for j in range(8):
+            turned = pltpu.roll(outer_ref[g * 8 + j], (16 * j + 8) % SLAB, 1)
+            block = jnp.where((lane >= 16 * j) & (lane < 16 * j + 16), turned, block)
+        pack[pl.ds(pl.multiple_of(g * SLAB, SLAB), SLAB)] = jnp.transpose(block)
+        return carry
+
+    lax.fori_loop(0, CH // 8, edges, 0)
+
+    def packed(p):
+        return pl.ds((p + 8) % 16, CH, stride=16)
+
+    for p in range(16):
+        edge_ref[p] = pack[packed(p), :]
     m_edge(0).start()
     m_edge(1).start()
 
@@ -215,12 +262,6 @@
             ab[k] = strip[1]
         for j in range(1, 16):
             m_first(j).start()
-
-    for k in range(8):
-        local_mat(ham_hbm, hg, k, ls.at[16 + k]).start()
-        remote_mat(ham_hbm, hg, k, 1).start()
-    cout = pltpu.make_async_copy(outer_hbm, outer_ref, ls.at[1])
-    cout.start()
 
     for k in range(8):
         cols = own_cols(k, c)
@@ -239,15 +280,22 @@
     tl[8:16] = edge_ref[0:8]
     tr[0:8] = edge_ref[8:16]
 
-    col_upper = par_ref[CH:CH + 1, :]
-    col_lower = par_ref[CH + 1:CH + 2, :]
+    def doubled(x):
+        return jnp.concatenate([x, x], axis=1)
+
+    def coupled_field(b):
+        row = link_ref[pl.ds(jnp.clip(b, 0, 6), 1), :].astype(F32) * field_ref[...]
+        return doubled(jnp.where((b >= 0) & (b < 7), row, 0.0))
+
+    col_upper = coupled_field(s)
+    col_lower = coupled_field(s - 1)
     pos_lane = (lax.broadcasted_iota(jnp.int32, (1, SLAB), 1) + r * SLAB).astype(F32)
     lane_inv = charge / (radius_start + spacing * pos_lane)
 
     def outer_channel(ch):
         w = outer_ref[ch]
         acc = w
-        mid = (S0 + par_ref[pl.ds(ch, 1), :]) - lane_inv
+        mid = (S0 + thr_col[pl.ds(ch, 1), :]) - lane_inv
         for k in range(1, TERMS + 1):
             p1 = jnp.where(lane >= 1, pltpu.roll(w, 1, 1), 0.0)
             p2 = jnp.where(lane >= 2, pltpu.roll(w, 2, 1), 0.0)
@@ -277,8 +325,12 @@
         for pair in range(4):
             prod = jnp.dot(both, dc[:, pair * 768:(pair + 1) * 768], preferred_element_type=F32)
             for j in range(2):
-                pt[o, pair * 2 + j] = prod[:, j * ROWS:(j + 1) * ROWS].astype(BF)
-                m_low(o, pair * 2 + j).start()
+                k = pair * 2 + j
+                pt[o, k // 4, k % 4] = prod[:, j * ROWS:(j + 1) * ROWS].astype(BF)
+        for d in range(2):
+            m_far(o, d).start()
+        for d in range(2):
+            m_near(o, d).start()
 
         for d in range(2):
             wr(o, uo.at[o, xh, zz(d, -1)], 1 + d)
@@ -296,13 +348,18 @@
         m_f2(o, 2).start()
         for x in range(2):
             m_f2u(o, 2, x).start()
+        for d in range(2):
+            wr(o, rfar.at[o, d], 22 + d)
+            rows = slice(d * half, (d + 1) * half)
+            for x in range(2):
+                pt[o, x, zz(d), rows] = (pt[o, x, zz(d), rows].astype(F32) + rfar[o, d, x].astype(F32)).astype(BF)
+            m_both(o, d).start()
 
         @pl.when(o == 0)
         def _():
             for k in range(8):
                 local_mat(ham_hbm, hg, k, ls.at[16 + k]).wait()
                 remote_mat(ham_hbm, hg, k, 1).wait_recv()
-            cout.wait()
             m_edge(0).wait_recv()
             m_edge(1).wait_recv()
 
@@ -312,10 +369,26 @@
 
         lax.fori_loop(0, 6, chans, 0)
 
+        @pl.when(o == TERMS - 1)
+        def _():
+            pltpu.make_async_copy(outer_ref, outer_out, ls.at[1]).start()
+
+        near_cols = pl.ds(pl.multiple_of(xh * (KHALF // 2), KHALF // 2), KHALF // 2)
+        far_cols = pl.ds(pl.multiple_of((1 - xh) * (KHALF // 2), KHALF // 2), KHALF // 2)
+        acc[...] = jnp.dot(hg[:, near_cols], uo[o, xh].reshape(KHALF // 2, Q), preferred_element_type=F32)
+
+        for d in range(2):
+            wr(o, rz.at[o, d, :, part[1 - d]], 27 + d)
+            wr(o, rz.at[o, d, :, part[d]], 32 + d)
+        for x in range(2):
+            low = pt[o, x, z].astype(F32) + rz[o, 0, x].astype(F32) + rz[o, 1, x].astype(F32)
+            rsum[o, x] = low.astype(BF)
+            m_lowx(o, x).start()
+
         for d in range(3):
             wr(o, uo.at[o, 1 - xh, zz(d, -1), lo], 7 + d)
             wr(o, uo.at[o, 1 - xh, zz(d, -1), hi], 10 + d)
-        prod = jnp.dot(hg[...], uo[o].reshape(KHALF, Q), preferred_element_type=F32)
+        prod = acc[...] + jnp.dot(hg[:, far_cols], uo[o, 1 - xh].reshape(KHALF // 2, Q), preferred_element_type=F32)
         gpart = prod[768:816] + prod[816:864]
         for j in range(2):
             hp[o, j, 0:ROWS] = prod[j * ROWS:(j + 1) * ROWS]
@@ -367,12 +440,15 @@
         ct[0:8] = ct[0:8] + dl[2:10]
         ct[8:16] = ct[8:16] + dr[2:10]
 
-        for k in range(8):
-            wr(o, rl.at[o, k], 22 + k)
-        low = rl[o, 0].astype(F32)
-        for k in range(1, 8):
-            low = low + rl[o, k].astype(F32)
-        low = jnp.transpose(low)
+        @pl.when(o == TERMS - 1)
+        def _():
+            for p in range(16):
+                pack[packed(p), :] = ct[p]
+            pltpu.make_async_copy(pack, pack_hbm, ls.at[2]).start()
+
+        for x in range(2):
+            wr(o, rl.at[o, x], 25 + x)
+        low = jnp.transpose(rl[o, 0].astype(F32) + rl[o, 1].astype(F32))
         wr(o, ur.at[o], 31)
         img = (
             hp[o, c, 0:ROWS] + hr[o, 0:ROWS] + source
@@ -386,13 +462,8 @@
 
     lax.fori_loop(0, TERMS, order, 0)
 
-    def fix(ch, carry):
-        rows = ct[:, pl.ds(ch, 1), :].reshape(16, Q)
-        block = jnp.concatenate([rows[0:8], jnp.zeros((SLAB - 16, Q), F32), rows[8:16]], axis=0)
-        outer_ref[ch] = outer_ref[ch] + jnp.transpose(block)
-        return carry
-
-    lax.fori_loop(0, CH, fix, 0)
+    cend = pltpu.make_async_copy(total_ref, total_hbm, ls.at[0])
+    cend.start()
 
     def drain(o, carry):
         for m in all_msgs(o):
@@ -405,6 +476,9 @@
         remote_mat(ham_hbm, hg, k, 1).wait_send()
     m_edge(0).wait_send()
     m_edge(1).wait_send()
+    pltpu.make_async_copy(outer_ref, outer_out, ls.at[1]).wait()
+    pltpu.make_async_copy(pack, pack_hbm, ls.at[2]).wait()
+    cend.wait()
 
     @pl.when(r == 0)
     def _():
@@ -412,39 +486,51 @@
             m_first(j).wait_send()
 
 
+def finish(total_ref, outer_ref, pack_ref, inner_out, outer_out):
+    inner_out[...] = total_ref[...]
+    lane = lax.broadcasted_iota(jnp.int32, (1, SLAB), 1)
+    block = jnp.transpose(pack_ref[...])
+    for j in range(8):
+        turned = pltpu.roll(block, (SLAB - 16 * j - 8) % SLAB, 1)
+        outer_out[j] = outer_ref[j] + jnp.where((lane < 8) | (lane >= SLAB - 8), turned, 0.0)
+
+
 def per_device(
     inner_state, outer_state, block_hamiltonian, dipole, field_strength, dipole_links,
     ghost_amplitude, surface_amplitude, state_channel, threshold,
 ):
-    block_index = lax.axis_index("sym")
-    links = jnp.pad(dipole_links.astype(F32), ((1, 1), (0, 0)))
-    near = lax.dynamic_slice_in_dim(links, block_index, 2, 0)
-    near = near[::-1] * field_strength[None, :]
-    par = jnp.concatenate([
-        jnp.broadcast_to(threshold[0][:, None], (CH, Q)),
-        jnp.concatenate([near, near], axis=1),
-        jnp.zeros((6, Q), F32),
-    ], axis=0)
-    outer = outer_state[0]
-    edge = jnp.transpose(jnp.concatenate([outer[..., :8], outer[..., SLAB - 8:]], axis=-1), (2, 0, 1))
     any_ = pl.BlockSpec(memory_space=pl.ANY)
-    vmem = pl.BlockSpec(memory_space=pltpu.VMEM)
     dma = pltpu.SemaphoreType.DMA
-    inner_next, outer_next = pl.pallas_call(
+    total, outer, pack = pl.pallas_call(
         kernel,
         out_shape=(
             jax.ShapeDtypeStruct((ROWS, Q), F32),
             jax.ShapeDtypeStruct((CH, Q, SLAB), F32),
+            jax.ShapeDtypeStruct((CH * 16, Q), F32),
         ),
-        in_specs=[any_] * 4 + [vmem] * 5,
-        out_specs=(vmem, vmem),
+        in_specs=[any_] * 10,
+        out_specs=(any_,) * 3,
         scratch_shapes=[
+            pltpu.VMEM((1, Q // 2), F32),
+            pltpu.VMEM((7, Q // 2), jnp.int32),
+            pltpu.VMEM((1, CH), F32),
+            pltpu.VMEM((2, STATES), F32),
+            pltpu.VMEM((1, STATES), F32),
+            pltpu.VMEM((1, STATES), jnp.int32),
+            pltpu.VMEM((ROWS, Q), F32),
+            pltpu.VMEM((CH, Q, SLAB), F32),
+            pltpu.VMEM((16, CH, Q), F32),
+            pltpu.VMEM((CH * 16, Q), F32),
             pltpu.VMEM((ROWS, Q), F32),
             pltpu.VMEM((TERMS, 2, 4, ROWS, Q), BF),
             pltpu.VMEM((TERMS, 2, 4, ROWS, Q), BF),
             pltpu.VMEM((TERMS, Q, 2 * ROWS), BF),
-            pltpu.VMEM((TERMS, 8, Q, ROWS), BF),
-            pltpu.VMEM((TERMS, 8, Q, ROWS), BF),
+            pltpu.VMEM((TERMS, 2, 4, Q, ROWS), BF),
+            pltpu.VMEM((TERMS, 2, 2, Q // 2, ROWS), BF),
+            pltpu.VMEM((TERMS, 2, 2, Q, ROWS), BF),
+            pltpu.VMEM((TERMS, 2, Q, ROWS), BF),
+            pltpu.VMEM((TERMS, 2, Q, ROWS), BF),
+            pltpu.VMEM((864, Q), F32),
             pltpu.VMEM((TERMS, 2, ROWS + 48, Q), F32),
             pltpu.VMEM((TERMS, ROWS + 48, Q), F32),
             pltpu.VMEM((TERMS, 2, ROWS, Q), F32),
@@ -454,28 +540,42 @@
             pltpu.VMEM((ROWS, Q), F32),
             pltpu.VMEM((Q, Q), F32),
             pltpu.VMEM((16, CH, Q), F32),
+            pltpu.VMEM((CH, Q), F32),
+            pltpu.VMEM((16, CH, Q), F32),
             pltpu.VMEM((16, CH, Q), F32),
             pltpu.VMEM((12, CH, Q), F32),
             pltpu.VMEM((12, CH, Q), F32),
             pltpu.VMEM((12, CH, Q), F32),
-            pltpu.VMEM((16, CH, Q), F32),
             pltpu.VMEM((TERMS, CH, Q), F32),
             pltpu.VMEM((32, Q), F32),
             pltpu.VMEM((48, Q), F32),
-            dma((TERMS, 32)), dma((TERMS, 32)),
+            dma((TERMS, 34)), dma((TERMS, 34)),
             dma((2,)), dma((2,)),
             dma((16,)), dma,
             dma((2, 8)), dma((2, 8)),
             dma((24,)),
         ],
         compiler_params=pltpu.CompilerParams(
-            collective_id=0, has_side_effects=True, vmem_limit_bytes=52 * 1024 * 1024
+            collective_id=0, has_side_effects=True, vmem_limit_bytes=62 * 1024 * 1024
         ),
         name="propagate",
     )(
-        inner_state[0], outer, block_hamiltonian[0], dipole[0], par,
-        ghost_amplitude[0], surface_amplitude, state_channel, edge,
+        inner_state[0], outer_state[0], block_hamiltonian[0], dipole[0], field_strength[None],
+        dipole_links, threshold, ghost_amplitude[0], surface_amplitude, state_channel,
     )
+    rows_spec = pl.BlockSpec((ROWS // 3, Q), lambda i: (i, 0))
+    channels_spec = pl.BlockSpec((8, Q, SLAB), lambda i: (i, 0, 0))
+    inner_next, outer_next = pl.pallas_call(
+        finish,
+        grid=(CH // 8,),
+        out_shape=(
+            jax.ShapeDtypeStruct((ROWS, Q), F32),
+            jax.ShapeDtypeStruct((CH, Q, SLAB), F32),
+        ),
+        in_specs=[rows_spec, channels_spec, rows_spec],
+        out_specs=(rows_spec, channels_spec),
+        name="finish",
+    )(total, outer, pack)
     return inner_next[None], outer_next[None]
 
 

time: 168 us -> 111 us (0.66); the launches traced: 166 us -> 111 us
  Pallas kernels: 157 us -> 110 us
  local copies, waits for them, and re-layouts: 6.2 us -> 0 us
    pallas_call x1, Pallas kernels: 157 us -> 106 us  [per_device(): pl.pallas_call(kernel, out_shape=(jax.ShapeDtypeStruct((ROWS, Q), F32), j...]
    unnamed x11 -> x0, local copies, waits for them, and re-layouts: 5.4 us -> none
    pallas_call x0 -> x1, Pallas kernels: none -> 3.88 us  [per_device(): pl.pallas_call(finish, grid=(CH // 8,), out_shape=(jax.ShapeDtypeStruct((...]
where the time goes in v2:
time: 111 us
  Pallas kernels  110 us (99%)
    pallas_call x1, Pallas kernels, per_device(): pl.pallas_call(kernel, out_shape=(jax.ShapeDtypeStruct((ROWS, Q), F32), j...  106 us
    pallas_call x1, Pallas kernels, per_device(): pl.pallas_call(finish, grid=(CH // 8,), out_shape=(jax.ShapeDtypeStruct((...  3.88 us

profile of v2, /device:TPU:1, one launch (start us, length us, event | category | flops | bytes accessed | tf_op | source)
XLA Modules:
  0.0 110.8 jit_solution(474268264695320274)
XLA Ops:
  0.6 106.3 %propagate.1 = (f32[384,128]{1,0:T(8,128)}, f32[24,128,128]{2,1,0:T(8,128)}, f32[384,128]{1,0:T(8,128)}) custom-call(f32[384,128]{1,0:T(8,128)} %bitcast.11, f32[24,128,128]{2,1,0:T(8,128)} %bitcast.10, bf16[384,6144]{1,0:T(8,128)(2,1)} %bitcast.8, bf16[384,6144]{1,0:T(8,128)(2,1)} %bitcast.9, f32[1,64]{1,0:T(1,128)} %bitcast.13, s32[7,64]{1,0:T(8,128)} %rest_1_.1, ...), custom_call_target="tpu_custom_call" | custom-call | tf_op jit(solution)/shard_map/propagate/pallas_call | solution.py:504
  106.9 3.9 %finish.1 = (f32[384,128]{1,0:T(8,128)}, f32[24,128,128]{2,1,0:T(8,128)}) custom-call(f32[384,128]{1,0:T(8,128)} %get-tuple-element.7.total_ref, f32[24,128,128]{2,1,0:T(8,128)} %get-tuple-element.8.outer_ref, f32[384,128]{1,0:T(8,128)} %get-tuple-element.9.pack_ref), custom_call_target="tpu_custom_call" | custom-call | tf_op jit(solution)/shard_map/finish/pallas_call | solution.py:568

commit v3 on v2

--- a/solution.py
+++ b/solution.py
@@ -16,7 +16,8 @@
 F32 = jnp.float32
 
 ROWS = 384
-FIRST = 96
+FIRST = 48
+FIRST_UP = 192
 STATES = 6144
 KHALF = 3072
 CH = 24
@@ -30,12 +31,12 @@
 def kernel(
     inner_hbm, outer_hbm, ham_hbm, dip_hbm, *rest,
 ):
-    small_hbm, (total_hbm, outer_out, pack_hbm), scratch = rest[:6], rest[6:9], rest[9:]
+    small_hbm, (total_hbm, outer_out), scratch = rest[:6], rest[6:8], rest[8:]
     small, scratch = scratch[:6], scratch[6:]
     field_ref, link_ref, thr_ref, ghost_ref, surf_ref, chan_ref = small
     (
         total_ref, outer_ref, ct, pack,
-        uf, uo, uu, ut, pt, rfar, rz, rsum, rl, acc, hp, hr, up, ur, hg, dc, sh, slp,
+        uf, uo, uu, ut, pt, rfar, rz, rsum, rl, acc, accu, hp, hr, up, ur, hg, dc, sh, slp,
         edge_ref, thr_col, tl, tr, dl, dr, cs, ab, invr, ghs,
         ss, rs, es_s, es_r, as_s, as_r, ms_s, ms_r, ls,
     ) = scratch
@@ -104,17 +105,26 @@
 
     lo = pl.ds(0, FIRST)
     hi = pl.ds(FIRST, ROWS - FIRST)
+    lo_up = pl.ds(0, FIRST_UP)
+    hi_up = pl.ds(FIRST_UP, ROWS - FIRST_UP)
     ccol = pl.ds(pl.multiple_of(c * ROWS, ROWS), ROWS)
 
     def m_core(o):
         return rc(o, ut.at[o, :, ccol], ut.at[o, :, ccol], 0, 0, partner)
 
     def m_own(o, d):
-        ref = uo.at[o, xh, z]
+        ref = uo.at[o, xh, z, hi if d < 3 else lo]
         return rc(o, ref, ref, 1 + d, 1 + d, zdev[d] if d < 3 else xdev)
 
+    def m_own2(o, d):
+        ref = uo.at[o, xh, z, lo if d < 3 else hi]
+        return rc(o, ref, ref, 34 + d, 34 + d, zdev[d] if d < 3 else xdev)
+
     def m_up(o, x):
-        return rc(o, uo.at[o, xh, z], uu.at[o, xh, z], 5 + x, 5 + xh, dev(below, x, z))
+        return rc(o, uo.at[o, xh, z, lo_up], uu.at[o, xh, z, lo_up], 5 + x, 5 + xh, dev(below, x, z))
+
+    def m_up2(o, x):
+        return rc(o, uo.at[o, xh, z, hi_up], uu.at[o, xh, z, hi_up], 38 + x, 38 + xh, dev(below, x, z))
 
     def m_f1(o, d):
         ref = uo.at[o, 1 - xh, z, lo]
@@ -125,11 +135,11 @@
         return rc(o, ref, ref, 10 + d, 10 + d, xdev)
 
     def m_f2u(o, d, x):
-        return rc(o, uo.at[o, xh, zz(d, -1), hi], uu.at[o, xh, zz(d, -1), hi],
+        return rc(o, uo.at[o, xh, zz(d, -1), hi_up], uu.at[o, xh, zz(d, -1), hi_up],
                   13 + x * 3 + d, 13 + xh * 3 + d, dev(below, x, z))
 
     def m_f3(o, d):
-        ref = uu.at[o, :, z, lo]
+        ref = uu.at[o, :, z, lo_up]
         return rc(o, ref, ref, 19 + d, 19 + d, zdev[d])
 
     half = Q // 2
@@ -158,8 +168,8 @@
 
     def all_msgs(o):
         out = [m_core(o)]
-        out += [m_own(o, d) for d in range(4)]
-        out += [m_up(o, x) for x in range(2)]
+        out += [m(o, d) for d in range(4) for m in (m_own, m_own2)]
+        out += [m(o, x) for x in range(2) for m in (m_up, m_up2)]
         out += [m_f1(o, d) for d in range(3)] + [m_f2(o, d) for d in range(3)]
         out += [m_f2u(o, d, x) for x in range(2) for d in range(3)]
         out += [m_f3(o, d) for d in range(3)]
@@ -263,18 +273,6 @@
         for j in range(1, 16):
             m_first(j).start()
 
-    for k in range(8):
-        cols = own_cols(k, c)
-        hot = chan_ref[0:1, cols] == lax.broadcasted_iota(jnp.int32, (CH, ROWS), 0)
-        for j in range(2):
-            g = jnp.where(hot, ghost_ref[j:j + 1, cols], F32(0.0))
-            top = g.astype(BF)
-            hg[768 + j * CH:768 + (j + 1) * CH, k * ROWS:(k + 1) * ROWS] = top
-            hg[816 + j * CH:816 + (j + 1) * CH, k * ROWS:(k + 1) * ROWS] = (g - top.astype(F32)).astype(BF)
-    mine = pl.ds(pl.multiple_of(r * ROWS, ROWS), ROWS)
-    hot = chan_ref[0:1, mine] == lax.broadcasted_iota(jnp.int32, (Q, ROWS), 0)
-    sh[...] = jnp.transpose(jnp.where(hot, 0.5 * surf_ref[0:1, mine], F32(0.0)))
-    slp[...] = jnp.zeros_like(slp)
     for ref in (dl, dr, cs, ct):
         ref[...] = jnp.zeros_like(ref)
     tl[8:16] = edge_ref[0:8]
@@ -322,41 +320,66 @@
 
         wr(o, ut.at[o, :, ccol], 0)
         both = ut[o]
-        for pair in range(4):
-            prod = jnp.dot(both, dc[:, pair * 768:(pair + 1) * 768], preferred_element_type=F32)
-            for j in range(2):
-                k = pair * 2 + j
-                pt[o, k // 4, k % 4] = prod[:, j * ROWS:(j + 1) * ROWS].astype(BF)
+
+        def lower_for(zc):
+            for x in range(2):
+                cols = pl.ds(pl.multiple_of((x * 4 + zc) * ROWS, ROWS), ROWS)
+                pt[o, x, zc] = jnp.dot(both, dc[:, cols], preferred_element_type=F32).astype(BF)
+
+        lower_for(zz(2))
         for d in range(2):
             m_far(o, d).start()
+        for d in range(4):
+            m_own2(o, d).start()
+        for x in range(2):
+            m_up2(o, x).start()
         for d in range(2):
+            lower_for(zz(d))
             m_near(o, d).start()
 
-        for d in range(2):
-            wr(o, uo.at[o, xh, zz(d, -1)], 1 + d)
+        def pass_column(d):
+            wr(o, uo.at[o, xh, zz(d, -1), hi], 1 + d)
             m_f2(o, d).start()
+
+        def pass_column_down(d):
             for x in range(2):
                 m_f2u(o, d, x).start()
-        wr(o, uo.at[o, 1 - xh, z], 4)
+
+        pass_column(0)
+        pass_column(1)
+        pass_column_down(0)
+        pass_column_down(1)
+        wr(o, uo.at[o, 1 - xh, z, lo], 4)
         for d in range(3):
             m_f1(o, d).start()
-        for x in range(2):
-            wr(o, uu.at[o, x, z], 5 + x)
-        for d in range(3):
-            m_f3(o, d).start()
-        wr(o, uo.at[o, xh, zz(2, -1)], 3)
-        m_f2(o, 2).start()
-        for x in range(2):
-            m_f2u(o, 2, x).start()
+        pass_column(2)
+        pass_column_down(2)
         for d in range(2):
             wr(o, rfar.at[o, d], 22 + d)
             rows = slice(d * half, (d + 1) * half)
             for x in range(2):
                 pt[o, x, zz(d), rows] = (pt[o, x, zz(d), rows].astype(F32) + rfar[o, d, x].astype(F32)).astype(BF)
             m_both(o, d).start()
+        for x in range(2):
+            wr(o, uu.at[o, x, z, lo_up], 5 + x)
+        for d in range(3):
+            m_f3(o, d).start()
+        lower_for(z)
 
         @pl.when(o == 0)
         def _():
+            for k in range(8):
+                cols = own_cols(k, c)
+                hot = chan_ref[0:1, cols] == lax.broadcasted_iota(jnp.int32, (CH, ROWS), 0)
+                for j in range(2):
+                    g = jnp.where(hot, ghost_ref[j:j + 1, cols], F32(0.0))
+                    top = g.astype(BF)
+                    hg[768 + j * CH:768 + (j + 1) * CH, k * ROWS:(k + 1) * ROWS] = top
+                    hg[816 + j * CH:816 + (j + 1) * CH, k * ROWS:(k + 1) * ROWS] = (g - top.astype(F32)).astype(BF)
+            mine = pl.ds(pl.multiple_of(r * ROWS, ROWS), ROWS)
+            hot = chan_ref[0:1, mine] == lax.broadcasted_iota(jnp.int32, (Q, ROWS), 0)
+            sh[...] = jnp.transpose(jnp.where(hot, 0.5 * surf_ref[0:1, mine], F32(0.0)))
+            slp[...] = jnp.zeros_like(slp)
             for k in range(8):
                 local_mat(ham_hbm, hg, k, ls.at[16 + k]).wait()
                 remote_mat(ham_hbm, hg, k, 1).wait_recv()
@@ -369,12 +392,10 @@
 
         lax.fori_loop(0, 6, chans, 0)
 
-        @pl.when(o == TERMS - 1)
-        def _():
-            pltpu.make_async_copy(outer_ref, outer_out, ls.at[1]).start()
-
         near_cols = pl.ds(pl.multiple_of(xh * (KHALF // 2), KHALF // 2), KHALF // 2)
         far_cols = pl.ds(pl.multiple_of((1 - xh) * (KHALF // 2), KHALF // 2), KHALF // 2)
+        for d in range(3):
+            wr(o, uo.at[o, xh, zz(d, -1), lo], 34 + d)
         acc[...] = jnp.dot(hg[:, near_cols], uo[o, xh].reshape(KHALF // 2, Q), preferred_element_type=F32)
 
         for d in range(2):
@@ -385,10 +406,25 @@
             rsum[o, x] = low.astype(BF)
             m_lowx(o, x).start()
 
+        def cols_of(x, zc):
+            return pl.ds(pl.multiple_of((x * 4 + zc) * ROWS, ROWS), ROWS)
+
+        def add_own(zc):
+            acc[...] += jnp.dot(hg[:, cols_of(1 - xh, zc)], uo[o, 1 - xh, zc], preferred_element_type=F32)
+
+        def upper_of(x, zc):
+            return jnp.dot(dc[:, cols_of(x, zc)], uu[o, x, zc], preferred_element_type=F32)
+
+        wr(o, uo.at[o, 1 - xh, z, hi], 37)
+        add_own(z)
+        for x in range(2):
+            wr(o, uu.at[o, x, z, hi_up], 38 + x)
+        accu[...] = upper_of(0, z) + upper_of(1, z)
         for d in range(3):
             wr(o, uo.at[o, 1 - xh, zz(d, -1), lo], 7 + d)
             wr(o, uo.at[o, 1 - xh, zz(d, -1), hi], 10 + d)
-        prod = acc[...] + jnp.dot(hg[:, far_cols], uo[o, 1 - xh].reshape(KHALF // 2, Q), preferred_element_type=F32)
+            add_own(zz(d, -1))
+        prod = acc[...]
         gpart = prod[768:816] + prod[816:864]
         for j in range(2):
             hp[o, j, 0:ROWS] = prod[j * ROWS:(j + 1) * ROWS]
@@ -397,9 +433,10 @@
 
         for d in range(3):
             for x in range(2):
-                wr(o, uu.at[o, x, zz(d, -1), hi], 13 + x * 3 + d)
-            wr(o, uu.at[o, :, zz(d, -1), lo], 19 + d)
-        prod = jnp.dot(dc[...], uu[o].reshape(KHALF, Q), preferred_element_type=F32)
+                wr(o, uu.at[o, x, zz(d, -1), hi_up], 13 + x * 3 + d)
+            wr(o, uu.at[o, :, zz(d, -1), lo_up], 19 + d)
+            accu[...] += upper_of(0, zz(d, -1)) + upper_of(1, zz(d, -1))
+        prod = accu[...]
         for j in range(2):
             up[o, j] = prod[j * ROWS:(j + 1) * ROWS]
         m_upp(o).start()
@@ -444,7 +481,17 @@
         def _():
             for p in range(16):
                 pack[packed(p), :] = ct[p]
-            pltpu.make_async_copy(pack, pack_hbm, ls.at[2]).start()
+
+            def fix(g, carry):
+                block = jnp.transpose(pack[pl.ds(pl.multiple_of(g * SLAB, SLAB), SLAB)])
+                for j in range(8):
+                    turned = pltpu.roll(block, (SLAB - 16 * j - 8) % SLAB, 1)
+                    keep = jnp.where((lane < 8) | (lane >= SLAB - 8), turned, 0.0)
+                    outer_ref[g * 8 + j] = outer_ref[g * 8 + j] + keep
+                return carry
+
+            lax.fori_loop(0, CH // 8, fix, 0)
+            pltpu.make_async_copy(outer_ref, outer_out, ls.at[1]).start()
 
         for x in range(2):
             wr(o, rl.at[o, x], 25 + x)
@@ -477,7 +524,6 @@
     m_edge(0).wait_send()
     m_edge(1).wait_send()
     pltpu.make_async_copy(outer_ref, outer_out, ls.at[1]).wait()
-    pltpu.make_async_copy(pack, pack_hbm, ls.at[2]).wait()
     cend.wait()
 
     @pl.when(r == 0)
@@ -486,13 +532,20 @@
             m_first(j).wait_send()
 
 
-def finish(total_ref, outer_ref, pack_ref, inner_out, outer_out):
-    inner_out[...] = total_ref[...]
-    lane = lax.broadcasted_iota(jnp.int32, (1, SLAB), 1)
-    block = jnp.transpose(pack_ref[...])
-    for j in range(8):
-        turned = pltpu.roll(block, (SLAB - 16 * j - 8) % SLAB, 1)
-        outer_out[j] = outer_ref[j] + jnp.where((lane < 8) | (lane >= SLAB - 8), turned, 0.0)
+def finish(total_hbm, outer_hbm, inner_out, outer_out, total, outer, sems):
+    pairs = [(total_hbm, total, inner_out)]
+    for i in range(3):
+        part = pl.ds(i * 8, 8)
+        pairs.append((outer_hbm.at[part], outer.at[part], outer_out.at[part]))
+    loads = [pltpu.make_async_copy(a, b, sems.at[0, i]) for i, (a, b, _) in enumerate(pairs)]
+    stores = [pltpu.make_async_copy(b, c, sems.at[1, i]) for i, (_, b, c) in enumerate(pairs)]
+    for copy in loads:
+        copy.start()
+    for load, store in zip(loads, stores):
+        load.wait()
+        store.start()
+    for copy in stores:
+        copy.wait()
 
 
 def per_device(
@@ -501,15 +554,14 @@
 ):
     any_ = pl.BlockSpec(memory_space=pl.ANY)
     dma = pltpu.SemaphoreType.DMA
-    total, outer, pack = pl.pallas_call(
+    total, outer = pl.pallas_call(
         kernel,
         out_shape=(
             jax.ShapeDtypeStruct((ROWS, Q), F32),
             jax.ShapeDtypeStruct((CH, Q, SLAB), F32),
-            jax.ShapeDtypeStruct((CH * 16, Q), F32),
         ),
         in_specs=[any_] * 10,
-        out_specs=(any_,) * 3,
+        out_specs=(any_,) * 2,
         scratch_shapes=[
             pltpu.VMEM((1, Q // 2), F32),
             pltpu.VMEM((7, Q // 2), jnp.int32),
@@ -531,6 +583,7 @@
             pltpu.VMEM((TERMS, 2, Q, ROWS), BF),
             pltpu.VMEM((TERMS, 2, Q, ROWS), BF),
             pltpu.VMEM((864, Q), F32),
+            pltpu.VMEM((768, Q), F32),
             pltpu.VMEM((TERMS, 2, ROWS + 48, Q), F32),
             pltpu.VMEM((TERMS, ROWS + 48, Q), F32),
             pltpu.VMEM((TERMS, 2, ROWS, Q), F32),
@@ -549,7 +602,7 @@
             pltpu.VMEM((TERMS, CH, Q), F32),
             pltpu.VMEM((32, Q), F32),
             pltpu.VMEM((48, Q), F32),
-            dma((TERMS, 34)), dma((TERMS, 34)),
+            dma((TERMS, 40)), dma((TERMS, 40)),
             dma((2,)), dma((2,)),
             dma((16,)), dma,
             dma((2, 8)), dma((2, 8)),
@@ -563,19 +616,17 @@
         inner_state[0], outer_state[0], block_hamiltonian[0], dipole[0], field_strength[None],
         dipole_links, threshold, ghost_amplitude[0], surface_amplitude, state_channel,
     )
-    rows_spec = pl.BlockSpec((ROWS // 3, Q), lambda i: (i, 0))
-    channels_spec = pl.BlockSpec((8, Q, SLAB), lambda i: (i, 0, 0))
     inner_next, outer_next = pl.pallas_call(
         finish,
-        grid=(CH // 8,),
         out_shape=(
             jax.ShapeDtypeStruct((ROWS, Q), F32),
             jax.ShapeDtypeStruct((CH, Q, SLAB), F32),
         ),
-        in_specs=[rows_spec, channels_spec, rows_spec],
-        out_specs=(rows_spec, channels_spec),
+        in_specs=[any_] * 2,
+        out_specs=(any_,) * 2,
+        scratch_shapes=[pltpu.VMEM((ROWS, Q), F32), pltpu.VMEM((CH, Q, SLAB), F32), dma((2, 4))],
         name="finish",
-    )(total, outer, pack)
+    )(total, outer)
     return inner_next[None], outer_next[None]
 
 

time: 111 us -> 102 us (0.919)
  Pallas kernels: 110 us -> 101 us
    pallas_call x1, Pallas kernels: 106 us -> 98.4 us  [per_device(): pl.pallas_call(kernel, out_shape=(jax.ShapeDtypeStruct((ROWS, Q), F32), j...]
    pallas_call x1, Pallas kernels: 3.88 us -> 2.36 us  [per_device(): pl.pallas_call(finish, out_shape=(jax.ShapeDtypeStruct((ROWS, Q), F32), j...]
where the time goes in v3:
time: 102 us; the launch traced here: 101 us
  Pallas kernels  101 us (99%)
    pallas_call x1, Pallas kernels, per_device(): pl.pallas_call(kernel, out_shape=(jax.ShapeDtypeStruct((ROWS, Q), F32), j...  98.4 us
    pallas_call x1, Pallas kernels, per_device(): pl.pallas_call(finish, out_shape=(jax.ShapeDtypeStruct((ROWS, Q), F32), j...  2.36 us

profile of v3, /device:TPU:1, one launch (start us, length us, event | category | flops | bytes accessed | tf_op | source)
XLA Modules:
  0.0 101.4 jit_solution(4985398067860740542)
XLA Ops:
  0.6 98.4 %propagate.1 = (f32[384,128]{1,0:T(8,128)}, f32[24,128,128]{2,1,0:T(8,128)}) custom-call(f32[384,128]{1,0:T(8,128)} %bitcast.11, f32[24,128,128]{2,1,0:T(8,128)} %bitcast.10, bf16[384,6144]{1,0:T(8,128)(2,1)} %bitcast.8, bf16[384,6144]{1,0:T(8,128)(2,1)} %bitcast.9, f32[1,64]{1,0:T(1,128)} %bitcast.13, s32[7,64]{1,0:T(8,128)} %rest_1_.1, f32[1,24]{1,0:T(1,128)} %rest_2_.1, ...), custom_call_target="tpu_custom_call" | custom-call | tf_op jit(solution)/shard_map/propagate/pallas_call | solution.py:557
  99.0 2.4 %finish.1 = (f32[384,128]{1,0:T(8,128)}, f32[24,128,128]{2,1,0:T(8,128)}) custom-call(f32[384,128]{1,0:T(8,128)} %get-tuple-element.6.total_hbm, f32[24,128,128]{2,1,0:T(8,128)} %get-tuple-element.7.outer_hbm), custom_call_target="tpu_custom_call" | custom-call | tf_op jit(solution)/shard_map/finish/pallas_call | solution.py:619

commit v4 on v3

--- a/solution.py
+++ b/solution.py
@@ -349,9 +349,6 @@
         pass_column(1)
         pass_column_down(0)
         pass_column_down(1)
-        wr(o, uo.at[o, 1 - xh, z, lo], 4)
-        for d in range(3):
-            m_f1(o, d).start()
         pass_column(2)
         pass_column_down(2)
         for d in range(2):
@@ -360,6 +357,9 @@
             for x in range(2):
                 pt[o, x, zz(d), rows] = (pt[o, x, zz(d), rows].astype(F32) + rfar[o, d, x].astype(F32)).astype(BF)
             m_both(o, d).start()
+        wr(o, uo.at[o, 1 - xh, z, lo], 4)
+        for d in range(3):
+            m_f1(o, d).start()
         for x in range(2):
             wr(o, uu.at[o, x, z, lo_up], 5 + x)
         for d in range(3):

time: 102 us -> 101 us (level)
  no operation moved by 1% of the time
where the time goes in v4:
time: 101 us
  Pallas kernels  100 us (99%)
    pallas_call x1, Pallas kernels, per_device(): pl.pallas_call(kernel, out_shape=(jax.ShapeDtypeStruct((ROWS, Q), F32), j...  97.7 us
    pallas_call x1, Pallas kernels, per_device(): pl.pallas_call(finish, out_shape=(jax.ShapeDtypeStruct((ROWS, Q), F32), j...  2.36 us

profile of v4, /device:TPU:1, one launch (start us, length us, event | category | flops | bytes accessed | tf_op | source)
XLA Modules:
  0.0 100.7 jit_solution(16124722673546361550)
XLA Ops:
  0.6 97.7 %propagate.1 = (f32[384,128]{1,0:T(8,128)}, f32[24,128,128]{2,1,0:T(8,128)}) custom-call(f32[384,128]{1,0:T(8,128)} %bitcast.11, f32[24,128,128]{2,1,0:T(8,128)} %bitcast.10, bf16[384,6144]{1,0:T(8,128)(2,1)} %bitcast.8, bf16[384,6144]{1,0:T(8,128)(2,1)} %bitcast.9, f32[1,64]{1,0:T(1,128)} %bitcast.13, s32[7,64]{1,0:T(8,128)} %rest_1_.1, f32[1,24]{1,0:T(1,128)} %rest_2_.1, ...), custom_call_target="tpu_custom_call" | custom-call | tf_op jit(solution)/shard_map/propagate/pallas_call | solution.py:557
  98.3 2.4 %finish.1 = (f32[384,128]{1,0:T(8,128)}, f32[24,128,128]{2,1,0:T(8,128)}) custom-call(f32[384,128]{1,0:T(8,128)} %get-tuple-element.6.total_hbm, f32[24,128,128]{2,1,0:T(8,128)} %get-tuple-element.7.outer_hbm), custom_call_target="tpu_custom_call" | custom-call | tf_op jit(solution)/shard_map/finish/pallas_call | solution.py:619
